TPU v7x, 32 devices: a whole 2x2x4 slice. The times are simulated.
32 devices in a mesh: mode: 16 (over z, x, core), space: 2 (over y).
Axes of the slice: x: 2, y: 2, z: 4, core: 2. Of those that a mesh axis runs over, the one named last changes fastest.
Arguments:
- forward_fields: float32 [2, 48, 512, 512], P(None, 'mode', 'space'), may hold values from -30 to 30
- backward_fields: float32 [2, 48, 512, 512], P(None, 'mode', 'space'), may hold values from -30 to 30
- phase: float32 [512, 512], P('space'), may hold values from -3.140625 to 3.140625
Outputs:
- new_phase: float32 [512, 512], P('space')
All inputs are finite; a program needn't handle non-finite values.
Results may differ from a plain program's by a relative error of at most 0.0003.
Values sent between devices are 32-bit elements; how exact they have to be, the bound alone decides.
No kernel may reach another device: no remote copies, remote signals or barrier semaphores. Data moves between devices by JAX's collectives and lax.ppermute only.
A program may use at most 128 MiB of HBM per device.

v0:
```python
import math

import jax
import jax.numpy as jnp
import numpy as np
from jax import lax
from jax.experimental import pallas as pl
from jax.experimental.pallas import tpu as pltpu
from jax.sharding import PartitionSpec as P

gap_length = 0.02
wavelength = 1.55e-06
pixel_pitch = 8e-06
highest = lax.Precision.HIGHEST


def fourier_tables(pixels):
    indices = jnp.arange(pixels, dtype=jnp.int32)
    wrapped = indices[:, None] * indices[None, :] % pixels
    angles = 2.0 * math.pi / pixels * wrapped.astype(jnp.float32)
    return jnp.concatenate([jnp.cos(angles), jnp.sin(angles)], axis=1)


def transfer_block(pixels, first_column, col_width):
    indices = jnp.arange(pixels, dtype=jnp.int32)
    signed_rows = jnp.where(indices < pixels // 2, indices, indices - pixels).astype(jnp.float32)
    columns = first_column + jnp.arange(col_width, dtype=jnp.int32)
    signed_cols = jnp.where(columns < pixels // 2, columns, columns - pixels).astype(jnp.float32)
    squared = signed_rows[None, :] ** 2 + signed_cols[:, None] ** 2
    scaled = squared * (wavelength / (pixels * pixel_pitch)) ** 2
    angles = -2.0 * math.pi * (gap_length / wavelength) * scaled / (1.0 + jnp.sqrt(1.0 - scaled))
    return (jnp.cos(angles), jnp.sin(angles))


def rows_forward(fields, kernel, blocks):
    pixels = kernel.shape[0]
    rows_here = fields.shape[3]
    from_real = jnp.einsum("dkrx,xf->dkfr", fields[0], kernel, precision=highest)
    from_imag = jnp.einsum("dkrx,xf->dkfr", fields[1], kernel, precision=highest)
    spec_real = from_real[:, :, :pixels] + from_imag[:, :, pixels:]
    spec_imag = from_imag[:, :, :pixels] - from_real[:, :, pixels:]
    stacked = jnp.stack([spec_real, spec_imag])
    return stacked.reshape(
        2, fields.shape[1], fields.shape[2], blocks, pixels // blocks * rows_here
    )


def columns_section(column_data, kernel, cos_part, sin_part, directions, blocks):
    pixels = kernel.shape[0]
    rows_here = pixels // blocks
    col_width = column_data.shape[4] // rows_here
    depth = column_data.shape[1]
    items = column_data.shape[2]
    arranged = column_data.reshape(2, depth, items, blocks, col_width, rows_here)
    folded = kernel.reshape(blocks, rows_here, 2 * pixels)
    from_real = jnp.einsum("dkncr,nrf->dkcf", arranged[0], folded, precision=highest)
    from_imag = jnp.einsum("dkncr,nrf->dkcf", arranged[1], folded, precision=highest)
    freq_real = from_real[..., :pixels] + from_imag[..., pixels:]
    freq_imag = from_imag[..., :pixels] - from_real[..., pixels:]
    turned_sin = directions[:, None, None, None] * sin_part[None, None]
    moved_real = freq_real * cos_part - freq_imag * turned_sin
    moved_imag = freq_real * turned_sin + freq_imag * cos_part
    inverse_kernel = kernel.reshape(pixels, 2, blocks, rows_here)
    from_real = jnp.einsum("dkca,agnr->dkgncr", moved_real, inverse_kernel, precision=highest)
    from_imag = jnp.einsum("dkca,agnr->dkgncr", moved_imag, inverse_kernel, precision=highest)
    out_real = (from_real[:, :, 0] - from_imag[:, :, 1]) / pixels
    out_imag = (from_imag[:, :, 0] + from_real[:, :, 1]) / pixels
    stacked = jnp.stack([out_real, out_imag])
    return stacked.reshape(2, depth, items, blocks, col_width * rows_here)


def rows_inverse(column_data, kernel, blocks):
    pixels = kernel.shape[0]
    col_width = pixels // blocks
    rows_here = column_data.shape[4] // col_width
    arranged = column_data.reshape(
        2, column_data.shape[1], column_data.shape[2], blocks, col_width, rows_here
    )
    folded = kernel.reshape(blocks, col_width, 2 * pixels)
    from_real = jnp.einsum("dkncr,ncf->dkrf", arranged[0], folded, precision=highest)
    from_imag = jnp.einsum("dkncr,ncf->dkrf", arranged[1], folded, precision=highest)
    out_real = (from_real[..., :pixels] - from_imag[..., pixels:]) / pixels
    out_imag = (from_imag[..., :pixels] + from_real[..., pixels:]) / pixels
    return jnp.stack([out_real, out_imag])


def propagate(fields, directions, to_columns, to_rows, kernel, cos_part, sin_part, blocks):
    spectrum = rows_forward(fields, kernel, blocks)

    def column_work(column_data):
        return columns_section(column_data, kernel, cos_part, sin_part, directions, blocks)

    mixed = to_columns(spectrum, column_work)
    return rows_inverse(to_rows(mixed), kernel, blocks)


def phase_update(drive_real, drive_imag, phase):
    turned_imag = drive_real * jnp.sin(phase) + drive_imag * jnp.cos(phase)
    return phase - turned_imag / jnp.sqrt(drive_real * drive_real + drive_imag * drive_imag + 1.0)


def split_planes(forward_fields, backward_fields, phase):
    blocks = lax.axis_size("space")
    pixels = forward_fields.shape[3]
    per_device = forward_fields.shape[1]
    col_width = pixels // blocks
    kernel = fourier_tables(pixels)
    cos_part, sin_part = transfer_block(pixels, lax.axis_index("space") * col_width, col_width)
    arrived = propagate(
        forward_fields[:, None],
        jnp.ones((1,), jnp.float32),
        lambda payload, worker: worker(
            lax.all_to_all(payload, "space", split_axis=3, concat_axis=3, tiled=True)
        ),
        lambda payload: lax.all_to_all(payload, "space", split_axis=3, concat_axis=3, tiled=True),
        kernel,
        cos_part,
        sin_part,
        blocks,
    )[:, 0]
    returned = propagate(
        backward_fields[:, None],
        -jnp.ones((1,), jnp.float32),
        lambda payload, worker: worker(
            lax.all_to_all(payload, "space", split_axis=3, concat_axis=3, tiled=True)
        ),
        lambda payload: lax.all_to_all(payload, "space", split_axis=3, concat_axis=3, tiled=True),
        kernel,
        cos_part,
        sin_part,
        blocks,
    )[:, 0]
    product_real = returned[0] * arrived[0] + returned[1] * arrived[1]
    product_imag = returned[0] * arrived[1] - returned[1] * arrived[0]
    rotor_cos = jnp.cos(phase)
    rotor_sin = jnp.sin(phase)
    turn_real = product_real * rotor_cos - product_imag * rotor_sin
    turn_imag = product_real * rotor_sin + product_imag * rotor_cos
    local_real = jnp.sum(turn_real, axis=(1, 2)) / pixels
    local_imag = jnp.sum(turn_imag, axis=(1, 2)) / pixels
    local_power = jnp.sum(
        product_real * product_real + product_imag * product_imag, axis=(1, 2)
    ) / (pixels * pixels)
    correlation_real, correlation_imag, power_sum = lax.psum(
        (local_real, local_imag, local_power), "space"
    )
    inverse_norm = 1.0 / jnp.sqrt(
        correlation_real * correlation_real
        + correlation_imag * correlation_imag
        + power_sum
        + 1e-06
    )
    weight_real = (correlation_real * inverse_norm)[:, None, None]
    weight_imag = (-correlation_imag * inverse_norm)[:, None, None]
    drive_real = jnp.sum(weight_real * product_real - weight_imag * product_imag, axis=0)
    drive_imag = jnp.sum(weight_real * product_imag + weight_imag * product_real, axis=0)
    mode_root = math.sqrt(per_device * lax.axis_size("mode"))
    total_real, total_imag = lax.psum((drive_real, drive_imag), "mode")
    return phase_update(total_real / mode_root, total_imag / mode_root, phase)


def split_table(pixels):
    half = pixels // 2
    grid = np.outer(np.arange(half), np.arange(half)) % half
    angle = 2.0 * np.pi / half * grid
    cos, sin = np.cos(angle), np.sin(angle)
    matrix = np.block([[cos, -sin], [sin, cos]]).astype(np.float32)
    high = matrix.astype(jnp.bfloat16)
    low = (matrix - high.astype(np.float32)).astype(jnp.bfloat16)
    return np.stack([high, low])


def halves(value):
    high = value.astype(jnp.bfloat16)
    return high, (value - high.astype(jnp.float32)).astype(jnp.bfloat16)


def right_times(value, table):
    high, low = halves(value)
    left = jnp.concatenate([high, high, low], axis=1)
    right = jnp.concatenate([table[0], table[1], table[0]], axis=0)
    return jnp.dot(left, right, preferred_element_type=jnp.float32)


def left_times(table, value):
    high, low = halves(value)
    left = jnp.concatenate([table[0], table[1], table[0]], axis=1)
    right = jnp.concatenate([high, high, low], axis=0)
    return jnp.dot(left, right, preferred_element_type=jnp.float32)


def turn_back(real, imag, cos, sin):
    return real * cos + imag * sin, imag * cos - real * sin


def rows_kernel(plan, brought, index, matrix, turn, held, sems):
    rows = held.shape[2]
    blocks = plan[0][0].shape[2] // rows
    half = held.shape[3] // 2
    copies = [
        pltpu.make_async_copy(
            fields.at[:, index[at], pl.ds(i * rows, rows), :],
            held.at[n * blocks + i],
            sems.at[n * blocks + i],
        )
        for n, (fields, at, _, _) in enumerate(plan)
        for i in range(blocks)
    ]
    copies[0].start()
    for copy in brought:
        copy.start()
    for copy in copies[1:]:
        copy.start()
    for n, (_, _, even, odd) in enumerate(plan):
        for i in range(blocks):
            copies[n * blocks + i].wait()
            if n == 0 and i == 0:
                for copy in brought:
                    copy.wait()
            real, imag = held[n * blocks + i, 0], held[n * blocks + i, 1]
            sum_r, sum_i = real[:, :half] + real[:, half:], imag[:, :half] + imag[:, half:]
            odd_r, odd_i = turn_back(
                real[:, :half] - real[:, half:],
                imag[:, :half] - imag[:, half:],
                turn[0:1, :],
                turn[1:2, :],
            )
            stacked = jnp.concatenate(
                [
                    jnp.concatenate([sum_r, sum_i], axis=1),
                    jnp.concatenate([odd_r, odd_i], axis=1),
                ],
                axis=0,
            )
            result = right_times(stacked, matrix)
            to = pl.ds(i * rows, rows)
            even[0, to, :] = result[:rows, :half]
            even[1, to, :] = result[:rows, half:]
            odd[0, to, :] = result[rows:, :half]
            odd[1, to, :] = result[rows:, half:]


def columns_part(own, other, matrix, turned, turn_in, turn_out, cos_part, sin_part, sign, mixed):
    own_r, own_i = own[0], own[1]
    other_r, other_i = other[0], other[1]
    half, cols = own_r.shape

    def spread(value):
        return jnp.concatenate([value] * (cols // value.shape[1]), axis=1)

    odd_r, odd_i = turn_back(
        own_r - other_r, own_i - other_i, spread(turn_in[0]), spread(turn_in[1])
    )
    stacked = jnp.concatenate(
        [
            jnp.concatenate([own_r + other_r, odd_r], axis=1),
            jnp.concatenate([own_i + other_i, odd_i], axis=1),
        ],
        axis=0,
    )
    freq = left_times(turned, stacked)
    freq_r, freq_i = freq[:half], freq[half:]
    tc = jnp.concatenate([cos_part[0], cos_part[1]], axis=1)
    ts = jnp.concatenate([sin_part[0], sin_part[1]], axis=1)
    if sign < 0:
        moved_r, moved_i = freq_r * tc + freq_i * ts, freq_i * tc - freq_r * ts
    else:
        moved_r, moved_i = freq_r * tc - freq_i * ts, freq_i * tc + freq_r * ts
    back = left_times(matrix, jnp.concatenate([moved_r, moved_i], axis=0))
    even_r, even_i = back[:half, :cols], back[half:, :cols]
    odd_r, odd_i = back[:half, cols:], back[half:, cols:]
    cos, sin = spread(turn_out[0]), spread(turn_out[1])
    add_r, add_i = odd_r * cos - odd_i * sin, odd_i * cos + odd_r * sin
    mixed[0, :half, :] = even_r + add_r
    mixed[1, :half, :] = even_i + add_i
    mixed[0, half:, :] = even_r - add_r
    mixed[1, half:, :] = even_i - add_i


def rows_back(mixed_even, mixed_odd, turned, turn, rows):
    stacked = jnp.concatenate(
        [
            jnp.concatenate([mixed_even[0, rows, :], mixed_even[1, rows, :]], axis=1),
            jnp.concatenate([mixed_odd[0, rows, :], mixed_odd[1, rows, :]], axis=1),
        ],
        axis=0,
    )
    back = right_times(stacked, turned)
    block = back.shape[0] // 2
    half = back.shape[1] // 2
    even_r, even_i = back[:block, :half], back[:block, half:]
    odd_r, odd_i = back[block:, :half], back[block:, half:]
    cos, sin = turn[0:1, :], turn[1:2, :]
    add_r, add_i = odd_r * cos - odd_i * sin, odd_i * cos + odd_r * sin
    return (
        jnp.concatenate([even_r + add_r, even_r - add_r], axis=1),
        jnp.concatenate([even_i + add_i, even_i - add_i], axis=1),
    )


BLOCK = 128
WIDE = 256


def product_part(arr_r, arr_i, returned, phase_turn, product, rows, sums):
    ret_r, ret_i = returned[0, rows, :], returned[1, rows, :]
    pro_r, pro_i = ret_r * arr_r + ret_i * arr_i, ret_r * arr_i - ret_i * arr_r
    product[0, rows, :] = pro_r
    product[1, rows, :] = pro_i
    cos, sin = phase_turn[0, rows, :], phase_turn[1, rows, :]

    def fold(value):
        return jnp.sum(value.reshape(value.shape[0] // 8, 8, value.shape[1]), axis=0)

    return (
        sums[0] + fold(pro_r * cos - pro_i * sin),
        sums[1] + fold(pro_r * sin + pro_i * cos),
        sums[2] + fold(pro_r * pro_r + pro_i * pro_i),
    )


def weight_of(sums, pixels):
    def total(value):
        return jnp.sum(jnp.sum(value, axis=0, keepdims=True), axis=1, keepdims=True)

    cor_r, cor_i = total(sums[0]) / pixels, total(sums[1]) / pixels
    power = total(sums[2]) / (pixels * pixels)
    norm = 1.0 / jnp.sqrt(cor_r * cor_r + cor_i * cor_i + power + 1e-06)
    return cor_r * norm, -cor_i * norm


def back_kernel(
    own, other, matrix, turned, turn, turn_in, turn_out, cos_even, sin_even, cos_odd, sin_odd, out, mixed
):
    for e, (cos_part, sin_part) in enumerate(((cos_even, sin_even), (cos_odd, sin_odd))):
        columns_part(
            own.at[e], other.at[e], matrix, turned, turn_in, turn_out,
            cos_part, sin_part, -1, mixed.at[e],
        )

    def step(i, carry):
        rows = pl.ds(pl.multiple_of(i * BLOCK, BLOCK), BLOCK)
        real, imag = rows_back(mixed.at[0], mixed.at[1], turned, turn, rows)
        out[0, rows, :] = real
        out[1, rows, :] = imag
        return carry

    lax.fori_loop(0, out.shape[1] // BLOCK, step, 0)


def even_kernel(own, other, matrix, turned, turn_in, turn_out, cos_part, sin_part, out, mixed):
    columns_part(
        own, other, matrix, turned, turn_in, turn_out, cos_part, sin_part, 1, mixed
    )
    half = out.shape[2]
    for i in range(out.shape[1] // WIDE):
        rows = pl.ds(i * WIDE, WIDE)
        back = right_times(jnp.concatenate([mixed[0, rows, :], mixed[1, rows, :]], axis=1), turned)
        out[0, rows, :] = back[:, :half]
        out[1, rows, :] = back[:, half:]


def even_and_odd(even, mixed, turned, turn, rows):
    half = even.shape[2]
    back = right_times(jnp.concatenate([mixed[0, rows, :], mixed[1, rows, :]], axis=1), turned)
    odd_r, odd_i = back[:, :half], back[:, half:]
    cos, sin = turn[0:1, :], turn[1:2, :]
    add_r, add_i = odd_r * cos - odd_i * sin, odd_i * cos + odd_r * sin
    even_r, even_i = even[0, rows, :], even[1, rows, :]
    return (
        jnp.concatenate([even_r + add_r, even_r - add_r], axis=1),
        jnp.concatenate([even_i + add_i, even_i - add_i], axis=1),
    )


def last_kernel(
    flag, own, other, returned, phase_turn, matrix, turned, turn, turn_in, turn_out,
    cos_even, sin_even, cos_odd, sin_odd, out, mixed, product,
):
    pixels = returned.shape[1]
    for e, (cos_part, sin_part) in enumerate(((cos_even, sin_even), (cos_odd, sin_odd))):
        columns_part(
            own.at[e], other.at[e], matrix, turned, turn_in, turn_out,
            cos_part, sin_part, 1, mixed.at[e],
        )

    def step(i, sums):
        rows = pl.ds(pl.multiple_of(i * BLOCK, BLOCK), BLOCK)
        real, imag = rows_back(mixed.at[0], mixed.at[1], turned, turn, rows)
        return product_part(real, imag, returned, phase_turn, product, rows, sums)

    zero = jnp.zeros((8, pixels), jnp.float32)
    sums = lax.fori_loop(0, pixels // BLOCK, step, (zero, zero, zero))
    weight_r, weight_i = weight_of(sums, pixels)
    weight_r, weight_i = weight_r * flag[0], weight_i * flag[0]

    def apply(i, carry):
        rows = pl.ds(pl.multiple_of(i * 32, 32), 32)
        pro_r, pro_i = product[0, rows, :], product[1, rows, :]
        out[0, rows, :] = weight_r * pro_r - weight_i * pro_i
        out[1, rows, :] = weight_r * pro_i + weight_i * pro_r
        return carry

    lax.fori_loop(0, pixels // 32, apply, 0)


def final_kernel(
    place, own, other, even, returned, phase_turn, drive,
    matrix, turned, turn, turn_in, turn_out, cos_part, sin_part, sent_r, sent_i, far_r, far_i, mixed, product, kept_r, kept_i, sems,
):
    pixels = returned.shape[1]
    columns_part(
        own, other, matrix, turned, turn_in, turn_out, cos_part, sin_part, 1, mixed
    )

    def step(i, sums):
        rows = pl.ds(pl.multiple_of(i * WIDE, WIDE), WIDE)
        real, imag = even_and_odd(even, mixed, turned, turn, rows)
        return product_part(real, imag, returned, phase_turn, product, rows, sums)

    zero = jnp.zeros((8, pixels), jnp.float32)
    sums = lax.fori_loop(0, pixels // WIDE, step, (zero, zero, zero))
    weight_r, weight_i = weight_of(sums, pixels)
    part = pixels // 4

    for out_r, out_i, core in ((kept_r, kept_i, place[0]), (sent_r, sent_i, 1 - place[0])):
        for s in range(2):

            def apply(i, carry, s=s, out_r=out_r, out_i=out_i, core=core):
                rows = pl.ds(pl.multiple_of((2 * s + core) * part + i * 32, 32), 32)
                to = pl.ds(pl.multiple_of(i * 32, 32), 32)
                pro_r, pro_i = product[0, rows, :], product[1, rows, :]
                out_r[s, to, :] = drive[0, rows, :] + (weight_r * pro_r - weight_i * pro_i)
                out_i[s, to, :] = drive[1, rows, :] + (weight_r * pro_i + weight_i * pro_r)
                return carry

            lax.fori_loop(0, part // 32, apply, 0)
        if out_r is kept_r:
            leaving = [
                pltpu.make_async_copy(kept_r, far_r, sems.at[0]),
                pltpu.make_async_copy(kept_i, far_i, sems.at[1]),
            ]
            for copy in leaving:
                copy.start()
    for copy in leaving:
        copy.wait()


def in_vmem(count):
    return [pl.BlockSpec(memory_space=pltpu.VMEM) for _ in range(count)]


def in_smem():
    return pl.BlockSpec(memory_space=pltpu.SMEM)


def limit(mebibytes):
    return pltpu.CompilerParams(vmem_limit_bytes=mebibytes * 1024 * 1024)


ROWS_LIMIT = 24
FIELD_LIMIT = 30
FINAL_LIMIT = 20


def far(value):
    return pltpu.with_memory_space_constraint(value, pltpu.HBM)


def rows_call(index, sources, plan, matrix, turn, bring=False):
    _, _, rows, pixels = sources[0].shape
    half = pixels // 2
    whole = jax.ShapeDtypeStruct((2, 2, rows, half), jnp.float32)
    part = jax.ShapeDtypeStruct((2, rows, half), jnp.float32)
    shapes = [shape for _, joined in plan for shape in ([whole] if joined else [part, part])]
    count = len(sources)

    def kernel(index, *refs):
        fields, refs = refs[:count], refs[count:]
        matrix, turn, refs = refs[0], refs[1], refs[2:]
        outs, scratch = list(refs[: len(shapes)]), refs[len(shapes) :]
        brought = []
        if bring:
            near_matrix, near_turn, table_sems = scratch[2:]
            brought = [
                pltpu.make_async_copy(turn, near_turn, table_sems.at[0]),
                pltpu.make_async_copy(matrix, near_matrix, table_sems.at[1]),
            ]
            matrix, turn = near_matrix, near_turn
        entries = []
        for at, (source, joined) in enumerate(plan):
            if joined:
                out = outs.pop(0)
                entries.append((fields[source], at, out.at[0], out.at[1]))
            else:
                entries.append((fields[source], at, outs.pop(0), outs.pop(0)))
        rows_kernel(entries, brought, index, matrix, turn, scratch[0], scratch[1])

    blocks = 2 * len(plan)
    scratch = [
        pltpu.VMEM((blocks, 2, rows // 2, pixels), jnp.float32),
        pltpu.SemaphoreType.DMA((blocks,)),
    ]
    table_specs = in_vmem(2)
    if bring:
        table_specs = [pl.BlockSpec(memory_space=pltpu.HBM)] * 2
        scratch += [
            pltpu.VMEM(matrix.shape, matrix.dtype),
            pltpu.VMEM(turn.shape, turn.dtype),
            pltpu.SemaphoreType.DMA((2,)),
        ]
        matrix, turn = far(matrix), far(turn)
    return pl.pallas_call(
        kernel,
        out_shape=tuple(shapes),
        in_specs=[in_smem()] + [pl.BlockSpec(memory_space=pltpu.HBM)] * count + table_specs,
        out_specs=tuple(in_vmem(len(shapes))),
        scratch_shapes=scratch,
        compiler_params=limit(ROWS_LIMIT),
        name="rows",
    )(index, *[far(source) for source in sources], matrix, turn)


def field_tables(tables):
    names = ("matrix", "turned", "turn", "turn_in", "turn_out", "cos_even", "sin_even", "cos_odd", "sin_odd")
    return [tables[name] for name in names]


def back_call(own, other, tables):
    half = own.shape[2]
    return pl.pallas_call(
        back_kernel,
        out_shape=jax.ShapeDtypeStruct((2, 2 * half, 2 * half), jnp.float32),
        in_specs=in_vmem(11),
        out_specs=in_vmem(1)[0],
        scratch_shapes=[pltpu.VMEM((2, 2, 2 * half, half), jnp.float32)],
        compiler_params=limit(FIELD_LIMIT),
        name="back",
    )(own, other, *field_tables(tables))


def even_call(own, other, tables):
    half = own.shape[1]
    return pl.pallas_call(
        even_kernel,
        out_shape=jax.ShapeDtypeStruct((2, 2 * half, half), jnp.float32),
        in_specs=in_vmem(8),
        out_specs=in_vmem(1)[0],
        scratch_shapes=[pltpu.VMEM((2, 2 * half, half), jnp.float32)],
        compiler_params=limit(FIELD_LIMIT),
        name="even",
    )(own, other, tables["matrix"], tables["turned"], tables["turn_in"],
      tables["turn_out"], tables["cos_even"], tables["sin_even"])


def last_call(flag, own, other, returned, phase_turn, tables):
    half = own.shape[2]
    return pl.pallas_call(
        last_kernel,
        out_shape=jax.ShapeDtypeStruct(returned.shape, jnp.float32),
        in_specs=[in_smem()] + in_vmem(13),
        out_specs=in_vmem(1)[0],
        scratch_shapes=[
            pltpu.VMEM((2, 2, 2 * half, half), jnp.float32),
            pltpu.VMEM(returned.shape, jnp.float32),
        ],
        compiler_params=limit(FIELD_LIMIT),
        name="last",
    )(flag.reshape(1), own, other, returned, phase_turn, *field_tables(tables))


def final_call(place, own, other, even, returned, phase_turn, drive, tables):
    pixels = returned.shape[1]
    part = jax.ShapeDtypeStruct((2, pixels // 4, pixels), jnp.float32)
    return pl.pallas_call(
        final_kernel,
        out_shape=(part,) * 2 + (pltpu.HBM(part.shape, part.dtype),) * 2,
        in_specs=[in_smem()] + in_vmem(13),
        out_specs=tuple(in_vmem(2)) + (pl.BlockSpec(memory_space=pltpu.HBM),) * 2,
        scratch_shapes=[
            pltpu.VMEM(even.shape, jnp.float32),
            pltpu.VMEM(returned.shape, jnp.float32),
            pltpu.VMEM(part.shape, part.dtype),
            pltpu.VMEM(part.shape, part.dtype),
            pltpu.SemaphoreType.DMA((2,)),
        ],
        compiler_params=limit(FINAL_LIMIT),
        name="final",
    )(place.reshape(1), own, other, even, returned, phase_turn, drive, tables["matrix"], tables["turned"],
      tables["turn"], tables["turn_in"], tables["turn_out"], tables["cos_odd"], tables["sin_odd"])


def circle(turns):
    quarters = 4.0 * turns
    nearest = jnp.round(quarters)
    angle = (quarters - nearest) * (0.5 * math.pi)
    square = angle * angle
    sin = 1.0 / 362880.0
    for term in (-1.0 / 5040.0, 1.0 / 120.0, -1.0 / 6.0, 1.0):
        sin = sin * square + term
    sin = sin * angle
    cos = -1.0 / 3628800.0
    for term in (1.0 / 40320.0, -1.0 / 720.0, 1.0 / 24.0, -0.5, 1.0):
        cos = cos * square + term
    count = nearest.astype(jnp.int32)
    swapped = (count & 1) == 1
    cos, sin = jnp.where(swapped, sin, cos), jnp.where(swapped, cos, sin)
    cos = jnp.where(((count + 1) & 2) == 2, -cos, cos)
    sin = jnp.where((count & 2) == 2, -sin, sin)
    return cos, sin


def turned_table(half):
    index = jnp.arange(half, dtype=jnp.int32)
    wrapped = index[:, None] * index[None, :] % half
    cos, sin = circle(wrapped.astype(jnp.float32) / half)
    value = jnp.concatenate(
        [jnp.concatenate([cos, sin], axis=1), jnp.concatenate([-sin, cos], axis=1)], axis=0
    )
    high = lax.reduce_precision(value, 8, 7)
    return jnp.stack([high.astype(jnp.bfloat16), (value - high).astype(jnp.bfloat16)])


def permuted_transfer(pixels, e):
    half = pixels // 2
    order = jnp.arange(2, dtype=jnp.int32)[:, None] + 2 * jnp.arange(half, dtype=jnp.int32)[None, :]
    signed = jnp.where(order < half, order, order - pixels).astype(jnp.float32)
    squared = signed[:, :, None] ** 2 + signed[e][None, None, :] ** 2
    scaled = squared * (wavelength / (pixels * pixel_pitch)) ** 2
    cos, sin = circle(-(gap_length / wavelength) * scaled / (1.0 + jnp.sqrt(1.0 - scaled)))
    return cos / (pixels * pixels), sin / (pixels * pixels)


def after(value, *others):
    return lax.optimization_barrier((value,) + others)[0]


def whole_modes(forward_fields, backward_fields, phase):
    pixels = forward_fields.shape[3]
    half = pixels // 2
    modes_here = forward_fields.shape[1]
    mode_size = lax.axis_size("mode")
    outer = mode_size // 4
    axes = ("mode", "space")
    mode_index = lax.axis_index("mode")
    space_index = lax.axis_index("space")
    core_index = mode_index % 2
    x_index = mode_index // 2 % 2
    z_index = mode_index // 4

    def flat(mode, space):
        return mode * 2 + space

    everyone = [(mode, space) for mode in range(mode_size) for space in range(2)]
    to_space = [(flat(m, s), flat(m, 1 - s)) for m, s in everyone]
    to_core = [(flat(m, s), flat(m ^ 1, s)) for m, s in everyone]
    to_x = [(flat(m, s), flat(m ^ 2, s)) for m, s in everyone]
    to_z = {j: [(flat(m, s), flat(m ^ (4 * j), s)) for m, s in everyone] for j in range(1, outer)}
    last_mode = [(flat(m, 1 - m % 2), flat(m, m % 2)) for m in range(mode_size)]

    def send(value, pairs):
        return lax.ppermute(value, axes, pairs)

    def swap_if(bit, value):
        return jnp.where(bit == 1, value[::-1], value)

    def by_z(value):
        shape = value.shape
        value = value.reshape((outer // 2, 2) + shape[1:])
        value = jnp.where(z_index % 2 == 1, value[:, ::-1], value)
        value = swap_if(z_index // 2, value)
        return value.reshape(shape)

    piece_rows = half // mode_size

    def share(value, bit, pairs):
        return swap_if(bit, jnp.stack([value, send(value, pairs)]))

    matrix = jnp.asarray(split_table(pixels))
    angle = 2.0 * np.pi / pixels * np.arange(half)
    turn = jnp.asarray(np.stack([np.cos(angle), np.sin(angle)]).astype(np.float32))

    last = jnp.full((), modes_here - 1, jnp.int32)
    both_fields = (backward_fields, forward_fields)
    (rows_last_backward,) = rows_call(
        last.reshape(1), (backward_fields,), ((0, True),), matrix, turn, True
    )
    got_last_backward = send(rows_last_backward, last_mode)
    quarter = half // 4
    part = lax.dynamic_slice_in_dim(
        phase, after(core_index * 2 + x_index, rows_last_backward) * quarter, quarter, axis=0
    )
    other_part = send(part, to_space)
    (rows_last_forward,) = rows_call(
        after(last, part).reshape(1), (forward_fields,), ((0, True),), matrix, turn
    )
    got_last_forward = send(rows_last_forward, last_mode)
    cos_even, sin_even = permuted_transfer(pixels, 0)
    cos_odd, sin_odd = permuted_transfer(pixels, 1)
    modes = jnp.stack([1 - space_index, 1 - space_index])
    sent_backward, sent_even, sent_odd = rows_call(
        after(modes, rows_last_forward), both_fields, ((0, True), (1, False)), matrix, turn
    )
    modes = jnp.stack([space_index, space_index])
    own_backward, own_even, own_odd = rows_call(
        after(modes, sent_odd), both_fields, ((0, True), (1, False)), matrix, turn
    )
    got_backward = send(sent_backward, to_space)
    got_even = send(sent_even, to_space)
    got_odd = send(sent_odd, to_space)

    other_part = after(other_part, own_odd)
    other_phase = share(share(other_part, x_index, to_x), core_index, to_core)
    whole_phase = swap_if(
        space_index, jnp.stack([phase, other_phase.reshape(half, pixels)])
    ).reshape(pixels, pixels)
    phase_turn = jnp.stack(circle(whole_phase * (0.5 / math.pi)))

    turn_out = jnp.broadcast_to(turn[:, :, None], (2, half, 128))
    tables = {
        "matrix": matrix,
        "turned": turned_table(half),
        "turn": turn,
        "turn_out": turn_out,
        "turn_in": turn_out * (1.0 - 2.0 * space_index.astype(jnp.float32)),
        "cos_even": cos_even,
        "sin_even": sin_even,
        "cos_odd": cos_odd,
        "sin_odd": sin_odd,
    }

    takes_last = jnp.where(space_index == core_index, 1.0, 0.0)
    returned = back_call(rows_last_backward, got_last_backward, tables)
    drive = last_call(
        takes_last, after(rows_last_forward, returned), got_last_forward, returned, phase_turn, tables
    )
    returned = back_call(after(own_backward, drive), got_backward, tables)
    even = even_call(after(own_even, returned), got_even, tables)
    sent_r, sent_i, kept_r, kept_i = final_call(
        core_index, own_odd, got_odd, even, returned, phase_turn, drive, tables
    )
    shape = (2, 2, outer, piece_rows, pixels)
    real = (kept_r + send(sent_r, to_core)).reshape(shape)
    imag = (kept_i + send(sent_i, to_core)).reshape(shape)

    def keep(value, axis, index):
        return lax.dynamic_index_in_dim(value, index, axis=axis, keepdims=False)

    def step(value, axis, index, pairs):
        return keep(value, axis, index) + send(keep(value, axis, 1 - index), pairs)

    real = step(real, 1, x_index, to_x)
    imag = step(imag, 0, space_index, to_space)
    real = step(real, 0, space_index, to_space)
    imag = step(imag, 0, x_index, to_x)
    both = by_z(jnp.stack([real, imag], axis=1))
    total = both[0]
    for j in range(1, outer):
        total = total + send(both[j], to_z[j])
    mode_root = math.sqrt(modes_here * mode_size)
    place = (core_index * 2 + x_index) * outer + z_index
    piece = lax.dynamic_slice_in_dim(phase, place * piece_rows, piece_rows, axis=0)
    updated = phase_update(total[0] / mode_root, total[1] / mode_root, piece)
    pieces = by_z(jnp.stack([updated] + [send(updated, to_z[j]) for j in range(1, outer)]))
    pieces = share(share(pieces, x_index, to_x), core_index, to_core)
    return pieces.reshape(half, pixels)


def on_device(forward_fields, backward_fields, phase):
    pixels = forward_fields.shape[3]
    if (
        lax.axis_size("space") == 2
        and lax.axis_size("mode") == 16
        and forward_fields.shape[1] == 3
        and pixels % 512 == 0
    ):
        return whole_modes(forward_fields, backward_fields, phase)
    return split_planes(forward_fields, backward_fields, phase)


def solution(mesh):
    in_specs = (P(None, "mode", "space", None), P(None, "mode", "space", None), P("space", None))
    out_specs = P("space", None)
    return jax.shard_map(
        on_device, mesh=mesh, in_specs=in_specs, out_specs=out_specs, check_vma=False
    )
```

profile of v0, /device:TPU:0, one launch (start us, length us, event | category | flops | bytes accessed | tf_op | source)
XLA Modules:
  0.0 143.1 jit_solution(1069818956063077666)
XLA Ops:
  0.0 3.7 %rows.4.own = f32[2,2,256,256]{3,2,1,0:T(8,128)} custom-call(s32[1]{0:T(128)} %constant.176.clone.1.index, f32[2,3,256,512]{3,2,1,0:T(8,128)} %refs_0_.7, bf16[2,512,512]{2,1,0:T(8,128)(2,1)} %constant.200.clone.refs_1_.refs_2_.matrix, f32[2,256]{1,0:T(2,128)} %constant.201.clone.refs_2_.refs_3_.turn), custom_call_target="tpu_custom_call" | custom-call | tf_op jit(solution)/shard_map/rows/pallas_call | solution.py:513
  3.8 1.3 collective-permute-start.1
  5.1 0.9 constant_dynamic-slice_fusion
  6.0 4.0 %collective-permute-start.3 = (f32[64,512]{1,0:T(8,128)S(1)}, f32[64,512]{1,0:T(8,128)S(1)}, u32[]{:S(2)}, u32[]{:S(2)}) collective-permute-start(f32[64,512]{1,0:T(8,128)S(1)} %constant_dynamic-slice_fusion), channel_id=1, source_target_pairs={{0,1},{1,0},{2,3},{3,2},{4,5},{5,4},{6,7},{7,6},{8,9},{9,8},{10,11... | collective-permute-start | bytes 393224 | tf_op jit(solution)/shard_map/ppermute | solution.py:662
  10.0 3.2 %rows.5.own = f32[2,2,256,256]{3,2,1,0:T(8,128)} custom-call(s32[1]{0:T(128)} %bitcast.3.index, f32[2,3,256,512]{3,2,1,0:T(8,128)} %refs_1_.5, bf16[2,512,512]{2,1,0:T(8,128)(2,1)S(1)} %copy-done, f32[2,256]{1,0:T(2,128)S(1)} %copy-done.9), custom_call_target="tpu_custom_call" | custom-call | tf_op jit(solution)/shard_map/rows/pallas_call | solution.py:513
  13.3 1.3 collective-permute-start.2
  14.6 5.0 %rows.6 = (f32[2,2,256,256]{3,2,1,0:T(8,128)S(1)}, f32[2,256,256]{2,1,0:T(8,128)}, f32[2,256,256]{2,1,0:T(8,128)}) custom-call(s32[2]{0:T(128)S(1)} %get-tuple-element.25.index, f32[2,3,256,512]{3,2,1,0:T(8,128)} %refs_0_.7, f32[2,3,256,512]{3,2,1,0:T(8,128)} %refs_1_.5, bf16[2,512,512]{2,1,0:T(8,128)(2,1)S(1)} %copy-done, f32[2,256]{1,0:T(2,128)S(1)} %copy-done.9), custom_call_target="tpu_custom_call" | custom-call | tf_op jit(solution)/shard_map/rows/pallas_call | solution.py:513
  19.6 1.0 copy-done.10
  20.6 3.6 %collective-permute-start.7 = (f32[2,256,256]{2,1,0:T(8,128)}, f32[2,256,256]{2,1,0:T(8,128)}, u32[]{:S(2)}, u32[]{:S(2)}) collective-permute-start(f32[2,256,256]{2,1,0:T(8,128)} %get-tuple-element.36), channel_id=1, source_target_pairs={{0,1},{1,0},{2,3},{3,2},{4,5},{5,4},{6,7},{7,6},{8,9},{9,8},{10,11... | collective-permute-start | bytes 1572872 | tf_op jit(solution)/shard_map/ppermute | solution.py:662
  24.7 0.4 negate_select_fusion.6
  25.2 4.0 %rows.7 = (f32[2,2,256,256]{3,2,1,0:T(8,128)S(1)}, f32[2,256,256]{2,1,0:T(8,128)S(1)}, f32[2,256,256]{2,1,0:T(8,128)S(1)}) custom-call(s32[2]{0:T(128)S(1)} %get-tuple-element.27.index, f32[2,3,256,512]{3,2,1,0:T(8,128)} %refs_0_.7, f32[2,3,256,512]{3,2,1,0:T(8,128)} %refs_1_.5, bf16[2,512,512]{2,1,0:T(8,128)(2,1)S(1)} %copy-done, f32[2,256]{1,0:T(2,128)S(1)} %copy-done.9), custom_call_target="tpu_custom_call" | custom-call | tf_op jit(solution)/shard_map/rows/pallas_call | solution.py:513
  29.2 2.9 %fusion.20 = (f32[2,256,256]{2,1,0:T(8,128)S(1)}, f32[2,256,256]{2,1,0:T(8,128)S(1)}, f32[2,256,256]{2,1,0:T(8,128)}, f32[2,256,256]{2,1,0:T(8,128)}) fusion(f32[256]{0:T(256)S(1)} %bitcast.121, f32[2,256]{1,0:T(2,128)S(1)} %fusion.41, f32[256]{0:T(256)S(1)} %bitcast.122), kind=kLoop, calls=%fused_computation.52 | loop fusion | flops 12058624 | bytes 2101248 | tf_op jit(solution)/shard_map/div | solution.py:631
  32.2 2.7 %collective-permute-start.4 = (f32[64,512]{1,0:T(8,128)S(1)}, f32[64,512]{1,0:T(8,128)S(1)}, u32[]{:S(2)}, u32[]{:S(2)}) collective-permute-start(f32[64,512]{1,0:T(8,128)S(1)} %collective-permute-done.3), channel_id=1, source_target_pairs={{0,4},{1,5},{2,6},{3,7},{4,0},{5,1},{6,2},{7,3},{8,12},{9,13},{10,... | collective-permute-start | bytes 393224 | tf_op jit(solution)/shard_map/ppermute | solution.py:662
  35.1 3.6 %collective-permute-done.4 = f32[64,512]{1,0:T(8,128)S(1)} collective-permute-done((f32[64,512]{1,0:T(8,128)S(1)}, f32[64,512]{1,0:T(8,128)S(1)}, u32[]{:S(2)}, u32[]{:S(2)}) %collective-permute-start.4) | collective-permute-done | bytes 131104 | tf_op jit(solution)/shard_map/ppermute | solution.py:662
  38.7 0.7 reverse_select_fusion.6
  39.6 1.7 %collective-permute-done.5 = f32[2,64,512]{2,1,0:T(8,128)} collective-permute-done((f32[2,64,512]{2,1,0:T(8,128)}, f32[2,64,512]{2,1,0:T(8,128)}, u32[]{:S(2)}, u32[]{:S(2)}) %collective-permute-start.5) | collective-permute-done | bytes 262176 | tf_op jit(solution)/shard_map/ppermute | solution.py:662
  41.4 1.1 collective-permute-start.6
  42.5 1.0 pad_maximum_fusion.4
  43.7 1.3 negate_select_fusion.1
  45.5 0.6 copy-done.1
  46.2 8.2 %back.2.returned = f32[2,512,512]{2,1,0:T(8,128)S(1)} custom-call(f32[2,2,256,256]{3,2,1,0:T(8,128)} %rows.4.own, f32[2,2,256,256]{3,2,1,0:T(8,128)} %collective-permute-done.1.other, bf16[2,512,512]{2,1,0:T(8,128)(2,1)S(1)} %copy-done, bf16[2,512,512]{2,1,0:T(8,128)(2,1)S(1)} %pad_maximum_fusion.2.turned, f32[2,256]{1,0:T(2,128)S(1)} %copy-done.9, ...), custom_call_target="tpu_custom_call" | custom-call | tf_op jit(solution)/shard_map/back/pallas_call | solution.py:531
  54.5 9.2 %last.1.drive = f32[2,512,512]{2,1,0:T(8,128)S(1)} custom-call(f32[1]{0:T(128)} %bitcast.4.flag, f32[2,2,256,256]{3,2,1,0:T(8,128)} %rows.5.own, f32[2,2,256,256]{3,2,1,0:T(8,128)} %collective-permute-done.2.other, f32[2,512,512]{2,1,0:T(8,128)S(1)} %back.2.returned, f32[2,512,512]{2,1,0:T(8,128)S(1)} %pad_maximum_fusion.phase_turn, ...), custom_call_target="tpu_custom_call" | custom-call | tf_op jit(solution)/shard_map/last/pallas_call | solution.py:558
  63.7 16.3 %collective-permute-done.6.other = f32[2,2,256,256]{3,2,1,0:T(8,128)S(1)} collective-permute-done((f32[2,2,256,256]{3,2,1,0:T(8,128)}, f32[2,2,256,256]{3,2,1,0:T(8,128)S(1)}, u32[]{:S(2)}, u32[]{:S(2)}) %collective-permute-start.6) | collective-permute-done | bytes 1048608 | tf_op jit(solution)/shard_map/ppermute | solution.py:662
  80.0 6.5 %back.3.returned = f32[2,512,512]{2,1,0:T(8,128)S(1)} custom-call(f32[2,2,256,256]{3,2,1,0:T(8,128)S(1)} %copy-done.4, f32[2,2,256,256]{3,2,1,0:T(8,128)S(1)} %collective-permute-done.6.other, bf16[2,512,512]{2,1,0:T(8,128)(2,1)S(1)} %copy-done, bf16[2,512,512]{2,1,0:T(8,128)(2,1)S(1)} %pad_maximum_fusion.2.turned, f32[2,256]{1,0:T(2,128)S(1)} %copy-done.9, ...), custom_call_target="tpu_custom_call" | custom-call | tf_op jit(solution)/shard_map/back/pallas_call | solution.py:531
  86.6 4.2 %even.1 = f32[2,512,256]{2,1,0:T(8,128)S(1)} custom-call(f32[2,256,256]{2,1,0:T(8,128)S(1)} %copy-done.8, f32[2,256,256]{2,1,0:T(8,128)} %collective-permute-done.7.other, bf16[2,512,512]{2,1,0:T(8,128)(2,1)S(1)} %copy-done, bf16[2,512,512]{2,1,0:T(8,128)(2,1)S(1)} %pad_maximum_fusion.2.turned, f32[2,256,128]{2,1,0:T(8,128)S(1)} %broadcast_in_dim.4.turn_in, ...), custom_call_target="tpu_custom_call" | custom-call | tf_op jit(solution)/shard_map/even/pallas_call | solution.py:544
  90.8 7.3 %final.1 = (f32[2,128,512]{2,1,0:T(8,128)}, f32[2,128,512]{2,1,0:T(8,128)}, f32[2,128,512]{2,1,0:T(8,128)}, f32[2,128,512]{2,1,0:T(8,128)}) custom-call(s32[1]{0:T(128)} %bitcast.place, f32[2,256,256]{2,1,0:T(8,128)S(1)} %copy-done.6, f32[2,256,256]{2,1,0:T(8,128)} %collective-permute-done.other, f32[2,512,256]{2,1,0:T(8,128)S(1)} %even.1, ...), custom_call_target="tpu_custom_call" | custom-call | tf_op jit(solution)/shard_map/final/pallas_call | solution.py:575
  98.2 0.5 collective-permute-start.11
  98.7 1.6 %collective-permute-done.8 = f32[2,128,512]{2,1,0:T(8,128)S(1)} collective-permute-done((f32[2,128,512]{2,1,0:T(8,128)}, f32[2,128,512]{2,1,0:T(8,128)S(1)}, u32[]{:S(2)}, u32[]{:S(2)}) %collective-permute-start.8) | collective-permute-done | bytes 524320 | tf_op jit(solution)/shard_map/ppermute | solution.py:662
  100.3 1.1 add.1022
  101.5 2.7 %collective-permute-start.9 = (f32[2,4,16,512]{3,2,1,0:T(8,128)S(1)}, f32[2,4,16,512]{3,2,1,0:T(8,128)S(1)}, u32[]{:S(2)}, u32[]{:S(2)}) collective-permute-start(f32[2,4,16,512]{3,2,1,0:T(8,128)S(1)} %dynamic-slice_bitcast_fusion.1), channel_id=1, source_target_pairs={{0,4},{1,5},{2,6},{3,7},{4,0},{5,1},{6,2},{7,3},{8,12},{9,13},{10,... | collective-permute-start | bytes 786440 | tf_op jit(solution)/shard_map/ppermute | solution.py:662
  104.3 6.4 %collective-permute-done.9 = f32[2,4,16,512]{3,2,1,0:T(8,128)S(1)} collective-permute-done((f32[2,4,16,512]{3,2,1,0:T(8,128)S(1)}, f32[2,4,16,512]{3,2,1,0:T(8,128)S(1)}, u32[]{:S(2)}, u32[]{:S(2)}) %collective-permute-start.9) | collective-permute-done | bytes 262176 | tf_op jit(solution)/shard_map/ppermute | solution.py:662
  111.2 1.2 collective-permute-done.12
  112.9 3.0 %collective-permute-done.10 = f32[4,16,512]{2,1,0:T(8,128)S(1)} collective-permute-done((f32[4,16,512]{2,1,0:T(8,128)S(1)}, f32[4,16,512]{2,1,0:T(8,128)S(1)}, u32[]{:S(2)}, u32[]{:S(2)}) %collective-permute-start.10) | collective-permute-done | bytes 131104 | tf_op jit(solution)/shard_map/ppermute | solution.py:662
  115.9 1.6 %collective-permute-done.13 = f32[4,16,512]{2,1,0:T(8,128)S(1)} collective-permute-done((f32[4,16,512]{2,1,0:T(8,128)S(1)}, f32[4,16,512]{2,1,0:T(8,128)S(1)}, u32[]{:S(2)}, u32[]{:S(2)}) %collective-permute-start.13) | collective-permute-done | bytes 131104 | tf_op jit(solution)/shard_map/ppermute | solution.py:662
  117.6 1.7 %collective-permute-start.14 = (f32[2,16,512]{2,1,0:T(8,128)S(1)}, f32[2,16,512]{2,1,0:T(8,128)S(1)}, u32[]{:S(2)}, u32[]{:S(2)}) collective-permute-start(f32[2,16,512]{2,1,0:T(8,128)S(1)} %get-tuple-element.45), channel_id=1, source_target_pairs={{0,8},{1,9},{2,10},{3,11},{4,12},{5,13},{6,14},{7,15},{8,0},{9,1},... | collective-permute-start | bytes 196616 | tf_op jit(solution)/shard_map/ppermute | solution.py:662
  119.3 2.5 %collective-permute-start.16 = (f32[2,16,512]{2,1,0:T(8,128)S(1)}, f32[2,16,512]{2,1,0:T(8,128)S(1)}, u32[]{:S(2)}, u32[]{:S(2)}) collective-permute-start(f32[2,16,512]{2,1,0:T(8,128)S(1)} %get-tuple-element.46), channel_id=1, source_target_pairs={{0,24},{1,25},{2,26},{3,27},{4,28},{5,29},{6,30},{7,31},{8,16},{9,... | collective-permute-start | bytes 196616 | tf_op jit(solution)/shard_map/ppermute | solution.py:662
  121.8 0.8 collective-permute-done.14
  122.6 2.8 %collective-permute-done.16 = f32[2,16,512]{2,1,0:T(8,128)S(1)} collective-permute-done((f32[2,16,512]{2,1,0:T(8,128)S(1)}, f32[2,16,512]{2,1,0:T(8,128)S(1)}, u32[]{:S(2)}, u32[]{:S(2)}) %collective-permute-start.16) | collective-permute-done | bytes 65568 | tf_op jit(solution)/shard_map/ppermute | solution.py:662
  125.4 2.4 %collective-permute-done.15 = f32[2,16,512]{2,1,0:T(8,128)S(1)} collective-permute-done((f32[2,16,512]{2,1,0:T(8,128)S(1)}, f32[2,16,512]{2,1,0:T(8,128)S(1)}, u32[]{:S(2)}, u32[]{:S(2)}) %collective-permute-start.15) | collective-permute-done | bytes 65568 | tf_op jit(solution)/shard_map/ppermute | solution.py:662
  127.9 0.9 multiply_subtract_fusion
  128.8 1.4 collective-permute-start.19
  130.2 3.0 %collective-permute-start.17 = (f32[16,512]{1,0:T(8,128)S(1)}, f32[16,512]{1,0:T(8,128)S(1)}, u32[]{:S(2)}, u32[]{:S(2)}) collective-permute-start(f32[16,512]{1,0:T(8,128)S(1)} %multiply_subtract_fusion), channel_id=1, source_target_pairs={{0,8},{1,9},{2,10},{3,11},{4,12},{5,13},{6,14},{7,15},{8,0},{9,1},... | collective-permute-start | bytes 98312 | tf_op jit(solution)/shard_map/ppermute | solution.py:662
  133.2 1.3 collective-permute-done.19
  134.6 0.8 collective-permute-done.18
  135.5 0.7 collective-permute-start.20
  136.2 4.3 %collective-permute-done.20 = f32[4,16,512]{2,1,0:T(8,128)S(1)} collective-permute-done((f32[4,16,512]{2,1,0:T(8,128)S(1)}, f32[4,16,512]{2,1,0:T(8,128)S(1)}, u32[]{:S(2)}, u32[]{:S(2)}) %collective-permute-start.20) | collective-permute-done | bytes 131104 | tf_op jit(solution)/shard_map/ppermute | solution.py:662
  140.7 1.5 %collective-permute-done.21 = f32[2,4,16,512]{3,2,1,0:T(8,128)S(1)} collective-permute-done((f32[2,4,16,512]{3,2,1,0:T(8,128)S(1)}, f32[2,4,16,512]{3,2,1,0:T(8,128)S(1)}, u32[]{:S(2)}, u32[]{:S(2)}) %collective-permute-start.21) | collective-permute-done | bytes 262176 | tf_op jit(solution)/shard_map/ppermute | solution.py:662
  142.3 0.8 reverse_select_fusion.1
  (79 shorter events, 3.6 us)
Async XLA Ops:
  0.0 10.0 %copy-start = (bf16[2,512,512]{2,1,0:T(8,128)(2,1)S(1)}, bf16[2,512,512]{2,1,0:T(8,128)(2,1)}, u32[]{:S(2)}) copy-start(bf16[2,512,512]{2,1,0:T(8,128)(2,1)} %constant.200.clone.refs_1_.refs_2_.matrix) | copy-start | bytes 3145732
  0.0 10.0 %copy-start.9 = (f32[2,256]{1,0:T(2,128)S(1)}, f32[2,256]{1,0:T(2,128)}, u32[]{:S(2)}) copy-start(f32[2,256]{1,0:T(2,128)} %constant.201.clone.refs_2_.refs_3_.turn) | copy-start | bytes 6148
  3.8 41.4 %collective-permute-start.1 = (f32[2,2,256,256]{3,2,1,0:T(8,128)}, f32[2,2,256,256]{3,2,1,0:T(8,128)}, u32[]{:S(2)}, u32[]{:S(2)}) collective-permute-start(f32[2,2,256,256]{3,2,1,0:T(8,128)} %rows.4.own), channel_id=1, source_target_pairs={{1,0},{2,3},{5,4},{6,7},{9,8},{10,11},{13,12},{14,15},{17,16},{18,... | collective-permute-start | bytes 3145736 | tf_op jit(solution)/shard_map/ppermute | solution.py:662
  6.0 26.2 %collective-permute-start.3 = (f32[64,512]{1,0:T(8,128)S(1)}, f32[64,512]{1,0:T(8,128)S(1)}, u32[]{:S(2)}, u32[]{:S(2)}) collective-permute-start(f32[64,512]{1,0:T(8,128)S(1)} %constant_dynamic-slice_fusion), channel_id=1, source_target_pairs={{0,1},{1,0},{2,3},{3,2},{4,5},{5,4},{6,7},{7,6},{8,9},{9,8},{10,11... | collective-permute-start | bytes 393224 | tf_op jit(solution)/shard_map/ppermute | solution.py:662
  13.3 41.2 %collective-permute-start.2 = (f32[2,2,256,256]{3,2,1,0:T(8,128)}, f32[2,2,256,256]{3,2,1,0:T(8,128)}, u32[]{:S(2)}, u32[]{:S(2)}) collective-permute-start(f32[2,2,256,256]{3,2,1,0:T(8,128)} %rows.5.own), channel_id=1, source_target_pairs={{1,0},{2,3},{5,4},{6,7},{9,8},{10,11},{13,12},{14,15},{17,16},{18,... | collective-permute-start | bytes 3145736 | tf_op jit(solution)/shard_map/ppermute | solution.py:662
  19.6 1.0 copy-start.10
  20.6 65.9 %collective-permute-start.7 = (f32[2,256,256]{2,1,0:T(8,128)}, f32[2,256,256]{2,1,0:T(8,128)}, u32[]{:S(2)}, u32[]{:S(2)}) collective-permute-start(f32[2,256,256]{2,1,0:T(8,128)} %get-tuple-element.36), channel_id=1, source_target_pairs={{0,1},{1,0},{2,3},{3,2},{4,5},{5,4},{6,7},{7,6},{8,9},{9,8},{10,11... | collective-permute-start | bytes 1572872 | tf_op jit(solution)/shard_map/ppermute | solution.py:662
  24.2 66.5 %collective-permute-start = (f32[2,256,256]{2,1,0:T(8,128)}, f32[2,256,256]{2,1,0:T(8,128)}, u32[]{:S(2)}, u32[]{:S(2)}) collective-permute-start(f32[2,256,256]{2,1,0:T(8,128)} %get-tuple-element.26), channel_id=1, source_target_pairs={{0,1},{1,0},{2,3},{3,2},{4,5},{5,4},{6,7},{7,6},{8,9},{9,8},{10,11... | collective-permute-start | bytes 1572872 | tf_op jit(solution)/shard_map/ppermute | solution.py:662
  29.2 5.9 %copy-start.3 = (f32[2,2,256,256]{3,2,1,0:T(8,128)}, f32[2,2,256,256]{3,2,1,0:T(8,128)S(1)}, u32[]{:S(2)}) copy-start(f32[2,2,256,256]{3,2,1,0:T(8,128)S(1)} %get-tuple-element.33.own) | copy-start | bytes 3145732
  29.2 5.9 %copy-start.5 = (f32[2,256,256]{2,1,0:T(8,128)}, f32[2,256,256]{2,1,0:T(8,128)S(1)}, u32[]{:S(2)}) copy-start(f32[2,256,256]{2,1,0:T(8,128)S(1)} %get-tuple-element.28.own) | copy-start | bytes 1572868
  29.2 5.9 %copy-start.7 = (f32[2,256,256]{2,1,0:T(8,128)}, f32[2,256,256]{2,1,0:T(8,128)S(1)}, u32[]{:S(2)}) copy-start(f32[2,256,256]{2,1,0:T(8,128)S(1)} %get-tuple-element.35.own) | copy-start | bytes 1572868
  32.2 6.5 %collective-permute-start.4 = (f32[64,512]{1,0:T(8,128)S(1)}, f32[64,512]{1,0:T(8,128)S(1)}, u32[]{:S(2)}, u32[]{:S(2)}) collective-permute-start(f32[64,512]{1,0:T(8,128)S(1)} %collective-permute-done.3), channel_id=1, source_target_pairs={{0,4},{1,5},{2,6},{3,7},{4,0},{5,1},{6,2},{7,3},{8,12},{9,13},{10,... | collective-permute-start | bytes 393224 | tf_op jit(solution)/shard_map/ppermute | solution.py:662
  39.5 1.9 %collective-permute-start.5 = (f32[2,64,512]{2,1,0:T(8,128)}, f32[2,64,512]{2,1,0:T(8,128)}, u32[]{:S(2)}, u32[]{:S(2)}) collective-permute-start(f32[2,64,512]{2,1,0:T(8,128)} %reverse_select_fusion.6), channel_id=1, source_target_pairs={{0,2},{1,3},{2,0},{3,1},{4,6},{5,7},{6,4},{7,5},{8,10},{9,11},{10,... | collective-permute-start | bytes 786440 | tf_op jit(solution)/shard_map/ppermute | solution.py:662
  39.6 3.9 %copy-start.11 = (f32[256,512]{1,0:T(8,128)S(1)}, f32[256,512]{1,0:T(8,128)}, u32[]{:S(2)}) copy-start(f32[256,512]{1,0:T(8,128)} %param.7) | copy-start | bytes 1572868
  41.4 38.6 %collective-permute-start.6 = (f32[2,2,256,256]{3,2,1,0:T(8,128)}, f32[2,2,256,256]{3,2,1,0:T(8,128)S(1)}, u32[]{:S(2)}, u32[]{:S(2)}) collective-permute-start(f32[2,2,256,256]{3,2,1,0:T(8,128)} %copy-done.10), channel_id=1, source_target_pairs={{0,1},{1,0},{2,3},{3,2},{4,5},{5,4},{6,7},{7,6},{8,9},{9,8},{10,11... | collective-permute-start | bytes 3145736 | tf_op jit(solution)/shard_map/ppermute | solution.py:662
  45.0 1.0 copy-start.1
  45.0 1.2 copy-start.2
  54.4 25.6 %copy-start.4 = (f32[2,2,256,256]{3,2,1,0:T(8,128)S(1)}, f32[2,2,256,256]{3,2,1,0:T(8,128)}, u32[]{:S(2)}) copy-start(f32[2,2,256,256]{3,2,1,0:T(8,128)} %copy-done.3) | copy-start | bytes 3145732
  63.7 22.9 %copy-start.8 = (f32[2,256,256]{2,1,0:T(8,128)S(1)}, f32[2,256,256]{2,1,0:T(8,128)}, u32[]{:S(2)}) copy-start(f32[2,256,256]{2,1,0:T(8,128)} %copy-done.7) | copy-start | bytes 1572868
  86.5 4.2 %copy-start.6 = (f32[2,256,256]{2,1,0:T(8,128)S(1)}, f32[2,256,256]{2,1,0:T(8,128)}, u32[]{:S(2)}) copy-start(f32[2,256,256]{2,1,0:T(8,128)} %copy-done.5) | copy-start | bytes 1572868
  98.1 6.0 %copy-start.12 = (f32[2,128,512]{2,1,0:T(8,128)S(1)}, f32[2,128,512]{2,1,0:T(8,128)}, u32[]{:S(2)}) copy-start(f32[2,128,512]{2,1,0:T(8,128)} %get-tuple-element.39) | copy-start | bytes 1572868
  98.1 2.2 %collective-permute-start.8 = (f32[2,128,512]{2,1,0:T(8,128)}, f32[2,128,512]{2,1,0:T(8,128)S(1)}, u32[]{:S(2)}, u32[]{:S(2)}) collective-permute-start(f32[2,128,512]{2,1,0:T(8,128)} %get-tuple-element.38), channel_id=1, source_target_pairs={{0,2},{1,3},{2,0},{3,1},{4,6},{5,7},{6,4},{7,5},{8,10},{9,11},{10,... | collective-permute-start | bytes 1572872 | tf_op jit(solution)/shard_map/ppermute | solution.py:662
  98.2 5.9 %collective-permute-start.11 = (f32[2,128,512]{2,1,0:T(8,128)}, f32[2,128,512]{2,1,0:T(8,128)S(1)}, u32[]{:S(2)}, u32[]{:S(2)}) collective-permute-start(f32[2,128,512]{2,1,0:T(8,128)} %get-tuple-element.40), channel_id=1, source_target_pairs={{0,2},{1,3},{2,0},{3,1},{4,6},{5,7},{6,4},{7,5},{8,10},{9,11},{10,... | collective-permute-start | bytes 1572872 | tf_op jit(solution)/shard_map/ppermute | solution.py:662
  101.5 9.3 %collective-permute-start.9 = (f32[2,4,16,512]{3,2,1,0:T(8,128)S(1)}, f32[2,4,16,512]{3,2,1,0:T(8,128)S(1)}, u32[]{:S(2)}, u32[]{:S(2)}) collective-permute-start(f32[2,4,16,512]{3,2,1,0:T(8,128)S(1)} %dynamic-slice_bitcast_fusion.1), channel_id=1, source_target_pairs={{0,4},{1,5},{2,6},{3,7},{4,0},{5,1},{6,2},{7,3},{8,12},{9,13},{10,... | collective-permute-start | bytes 786440 | tf_op jit(solution)/shard_map/ppermute | solution.py:662
  104.3 8.1 %collective-permute-start.12 = (f32[2,4,16,512]{3,2,1,0:T(8,128)S(1)}, f32[2,4,16,512]{3,2,1,0:T(8,128)S(1)}, u32[]{:S(2)}, u32[]{:S(2)}) collective-permute-start(f32[2,4,16,512]{3,2,1,0:T(8,128)S(1)} %dynamic-slice_bitcast_fusion), channel_id=1, source_target_pairs={{0,1},{1,0},{2,3},{3,2},{4,5},{5,4},{6,7},{7,6},{8,9},{9,8},{10,11... | collective-permute-start | bytes 786440 | tf_op jit(solution)/shard_map/ppermute | solution.py:662
  110.8 5.0 %collective-permute-start.10 = (f32[4,16,512]{2,1,0:T(8,128)S(1)}, f32[4,16,512]{2,1,0:T(8,128)S(1)}, u32[]{:S(2)}, u32[]{:S(2)}) collective-permute-start(f32[4,16,512]{2,1,0:T(8,128)S(1)} %dynamic-slice_bitcast_fusion.3), channel_id=1, source_target_pairs={{0,1},{1,0},{2,3},{3,2},{4,5},{5,4},{6,7},{7,6},{8,9},{9,8},{10,11... | collective-permute-start | bytes 393224 | tf_op jit(solution)/shard_map/ppermute | solution.py:662
  112.5 5.0 %collective-permute-start.13 = (f32[4,16,512]{2,1,0:T(8,128)S(1)}, f32[4,16,512]{2,1,0:T(8,128)S(1)}, u32[]{:S(2)}, u32[]{:S(2)}) collective-permute-start(f32[4,16,512]{2,1,0:T(8,128)S(1)} %dynamic-slice_bitcast_fusion.2), channel_id=1, source_target_pairs={{0,4},{1,5},{2,6},{3,7},{4,0},{5,1},{6,2},{7,3},{8,12},{9,13},{10,... | collective-permute-start | bytes 393224 | tf_op jit(solution)/shard_map/ppermute | solution.py:662
  117.6 5.0 %collective-permute-start.14 = (f32[2,16,512]{2,1,0:T(8,128)S(1)}, f32[2,16,512]{2,1,0:T(8,128)S(1)}, u32[]{:S(2)}, u32[]{:S(2)}) collective-permute-start(f32[2,16,512]{2,1,0:T(8,128)S(1)} %get-tuple-element.45), channel_id=1, source_target_pairs={{0,8},{1,9},{2,10},{3,11},{4,12},{5,13},{6,14},{7,15},{8,0},{9,1},... | collective-permute-start | bytes 196616 | tf_op jit(solution)/shard_map/ppermute | solution.py:662
  119.3 6.2 %collective-permute-start.16 = (f32[2,16,512]{2,1,0:T(8,128)S(1)}, f32[2,16,512]{2,1,0:T(8,128)S(1)}, u32[]{:S(2)}, u32[]{:S(2)}) collective-permute-start(f32[2,16,512]{2,1,0:T(8,128)S(1)} %get-tuple-element.46), channel_id=1, source_target_pairs={{0,24},{1,25},{2,26},{3,27},{4,28},{5,29},{6,30},{7,31},{8,16},{9,... | collective-permute-start | bytes 196616 | tf_op jit(solution)/shard_map/ppermute | solution.py:662
  121.7 6.1 %collective-permute-start.15 = (f32[2,16,512]{2,1,0:T(8,128)S(1)}, f32[2,16,512]{2,1,0:T(8,128)S(1)}, u32[]{:S(2)}, u32[]{:S(2)}) collective-permute-start(f32[2,16,512]{2,1,0:T(8,128)S(1)} %get-tuple-element.47), channel_id=1, source_target_pairs={{0,16},{1,17},{2,18},{3,19},{4,20},{5,21},{6,22},{7,23},{8,24},{9,... | collective-permute-start | bytes 196616 | tf_op jit(solution)/shard_map/ppermute | solution.py:662
  128.8 5.8 %collective-permute-start.19 = (f32[16,512]{1,0:T(8,128)S(1)}, f32[16,512]{1,0:T(8,128)S(1)}, u32[]{:S(2)}, u32[]{:S(2)}) collective-permute-start(f32[16,512]{1,0:T(8,128)S(1)} %multiply_subtract_fusion), channel_id=1, source_target_pairs={{0,24},{1,25},{2,26},{3,27},{4,28},{5,29},{6,30},{7,31},{8,16},{9,... | collective-permute-start | bytes 98312 | tf_op jit(solution)/shard_map/ppermute | solution.py:662
  130.2 5.2 %collective-permute-start.18 = (f32[16,512]{1,0:T(8,128)S(1)}, f32[16,512]{1,0:T(8,128)S(1)}, u32[]{:S(2)}, u32[]{:S(2)}) collective-permute-start(f32[16,512]{1,0:T(8,128)S(1)} %multiply_subtract_fusion), channel_id=1, source_target_pairs={{0,16},{1,17},{2,18},{3,19},{4,20},{5,21},{6,22},{7,23},{8,24},{9,... | collective-permute-start | bytes 98312 | tf_op jit(solution)/shard_map/ppermute | solution.py:662
  130.2 5.3 %collective-permute-start.17 = (f32[16,512]{1,0:T(8,128)S(1)}, f32[16,512]{1,0:T(8,128)S(1)}, u32[]{:S(2)}, u32[]{:S(2)}) collective-permute-start(f32[16,512]{1,0:T(8,128)S(1)} %multiply_subtract_fusion), channel_id=1, source_target_pairs={{0,8},{1,9},{2,10},{3,11},{4,12},{5,13},{6,14},{7,15},{8,0},{9,1},... | collective-permute-start | bytes 98312 | tf_op jit(solution)/shard_map/ppermute | solution.py:662
  135.5 5.0 %collective-permute-start.20 = (f32[4,16,512]{2,1,0:T(8,128)S(1)}, f32[4,16,512]{2,1,0:T(8,128)S(1)}, u32[]{:S(2)}, u32[]{:S(2)}) collective-permute-start(f32[4,16,512]{2,1,0:T(8,128)S(1)} %bitcast.110), channel_id=1, source_target_pairs={{0,4},{1,5},{2,6},{3,7},{4,0},{5,1},{6,2},{7,3},{8,12},{9,13},{10,... | collective-permute-start | bytes 393224 | tf_op jit(solution)/shard_map/ppermute | solution.py:662
  140.6 1.6 %collective-permute-start.21 = (f32[2,4,16,512]{3,2,1,0:T(8,128)S(1)}, f32[2,4,16,512]{3,2,1,0:T(8,128)S(1)}, u32[]{:S(2)}, u32[]{:S(2)}) collective-permute-start(f32[2,4,16,512]{3,2,1,0:T(8,128)S(1)} %reverse_select_fusion.3), channel_id=1, source_target_pairs={{0,2},{1,3},{2,0},{3,1},{4,6},{5,7},{6,4},{7,5},{8,10},{9,11},{10,... | collective-permute-start | bytes 786440 | tf_op jit(solution)/shard_map/ppermute | solution.py:662
where the time goes:
time: 144 us; the launch traced here: 143 us
  Pallas kernels  51.4 us (36%)
  waiting for transfers between devices  49.6 us (34%)
  starting transfers between devices  27.6 us (19%)
  other arithmetic  10.9 us (8%)
  local copies, waits for them, and re-layouts  3.04 us (2%)
    ppermute x22, waiting for transfers between devices, send(): return lax.ppermute(value, axes, pairs)  49.6 us
    ppermute x22, starting transfers between devices, send(): return lax.ppermute(value, axes, pairs)  27.6 us
    pallas_call x4, Pallas kernels, rows_call(): pl.pallas_call(kernel, out_shape=tuple(shapes), in_specs=[in_smem()] + [p...  15.9 us
    pallas_call x2, Pallas kernels, back_call(): pl.pallas_call(back_kernel, out_shape=jax.ShapeDtypeStruct((2, 2 * half,...  14.7 us
    pallas_call x1, Pallas kernels, last_call(): pl.pallas_call(last_kernel, out_shape=jax.ShapeDtypeStruct(returned.shape...  9.21 us
    pallas_call x1, Pallas kernels, final_call(): pl.pallas_call(final_kernel, out_shape=(part,) * 2 + (pltpu.HBM(part.shap...  7.34 us
    pallas_call x1, Pallas kernels, even_call(): pl.pallas_call(even_kernel, out_shape=jax.ShapeDtypeStruct((2, 2 * half,...  4.19 us
    div x1, other arithmetic, permuted_transfer(): return (cos / (pixels * pixels), sin / (pixels * pixels))  2.88 us
  transfers between devices with their start and end apart: 22, of which 16 were waited for; matrix products, arithmetic and copies ran while one was open for 7% of the time, Pallas kernels for 28%

commit v1 on v0

--- a/solution.py
+++ b/solution.py
@@ -262,10 +262,11 @@
     freq_r, freq_i = freq[:half], freq[half:]
     tc = jnp.concatenate([cos_part[0], cos_part[1]], axis=1)
     ts = jnp.concatenate([sin_part[0], sin_part[1]], axis=1)
-    if sign < 0:
-        moved_r, moved_i = freq_r * tc + freq_i * ts, freq_i * tc - freq_r * ts
+    if isinstance(sign, int):
+        ts = ts if sign > 0 else -ts
     else:
-        moved_r, moved_i = freq_r * tc - freq_i * ts, freq_i * tc + freq_r * ts
+        ts = sign * ts
+    moved_r, moved_i = freq_r * tc - freq_i * ts, freq_i * tc + freq_r * ts
     back = left_times(matrix, jnp.concatenate([moved_r, moved_i], axis=0))
     even_r, even_i = back[:half, :cols], back[half:, :cols]
     odd_r, odd_i = back[:half, cols:], back[half:, cols:]
@@ -302,31 +303,23 @@
 WIDE = 256
 
 
+def add_sums(sums, pro_r, pro_i, cos, sin):
+    def fold(value):
+        return jnp.sum(value.reshape(value.shape[0] // 8, 8, value.shape[1]), axis=0)
+
+    return (
+        sums[0] + fold(pro_r * cos - pro_i * sin),
+        sums[1] + fold(pro_r * sin + pro_i * cos),
+        sums[2] + fold(pro_r * pro_r + pro_i * pro_i),
+    )
+
+
 def product_part(arr_r, arr_i, returned, phase_turn, product, rows, sums):
     ret_r, ret_i = returned[0, rows, :], returned[1, rows, :]
     pro_r, pro_i = ret_r * arr_r + ret_i * arr_i, ret_r * arr_i - ret_i * arr_r
     product[0, rows, :] = pro_r
     product[1, rows, :] = pro_i
-    cos, sin = phase_turn[0, rows, :], phase_turn[1, rows, :]
-
-    def fold(value):
-        return jnp.sum(value.reshape(value.shape[0] // 8, 8, value.shape[1]), axis=0)
-
-    return (
-        sums[0] + fold(pro_r * cos - pro_i * sin),
-        sums[1] + fold(pro_r * sin + pro_i * cos),
-        sums[2] + fold(pro_r * pro_r + pro_i * pro_i),
-    )
-
-
-def weight_of(sums, pixels):
-    def total(value):
-        return jnp.sum(jnp.sum(value, axis=0, keepdims=True), axis=1, keepdims=True)
-
-    cor_r, cor_i = total(sums[0]) / pixels, total(sums[1]) / pixels
-    power = total(sums[2]) / (pixels * pixels)
-    norm = 1.0 / jnp.sqrt(cor_r * cor_r + cor_i * cor_i + power + 1e-06)
-    return cor_r * norm, -cor_i * norm
+    return add_sums(sums, pro_r, pro_i, phase_turn[0, rows, :], phase_turn[1, rows, :])
 
 
 def back_kernel(
@@ -373,39 +366,62 @@
     )
 
 
-def last_kernel(
-    flag, own, other, returned, phase_turn, matrix, turned, turn, turn_in, turn_out,
-    cos_even, sin_even, cos_odd, sin_odd, out, mixed, product,
+def shared_kernel(
+    place, sign, own, other, matrix, turned, turn, turn_in, turn_out,
+    cos_even, sin_even, cos_odd, sin_odd, sent, kept, mixed,
 ):
-    pixels = returned.shape[1]
+    half = own.shape[2]
     for e, (cos_part, sin_part) in enumerate(((cos_even, sin_even), (cos_odd, sin_odd))):
         columns_part(
             own.at[e], other.at[e], matrix, turned, turn_in, turn_out,
-            cos_part, sin_part, 1, mixed.at[e],
+            cos_part, sin_part, sign[0], mixed.at[e],
         )
+    for out, first in ((sent, (1 - place[0]) * half), (kept, place[0] * half)):
+
+        def step(i, carry, out=out, first=first):
+            rows = pl.ds(pl.multiple_of(first + i * BLOCK, BLOCK), BLOCK)
+            to = pl.ds(pl.multiple_of(i * BLOCK, BLOCK), BLOCK)
+            real, imag = rows_back(mixed.at[0], mixed.at[1], turned, turn, rows)
+            out[0, to, :] = real
+            out[1, to, :] = imag
+            return carry
+
+        lax.fori_loop(0, half // BLOCK, step, 0)
+
+
+def totals(sums, pixels):
+    def total(value):
+        return jnp.sum(jnp.sum(value, axis=0, keepdims=True), axis=1, keepdims=True)
+
+    return total(sums[0]) / pixels, total(sums[1]) / pixels, total(sums[2]) / (pixels * pixels)
+
+
+def weight_of(cor_r, cor_i, power):
+    norm = 1.0 / jnp.sqrt(cor_r * cor_r + cor_i * cor_i + power + 1e-06)
+    return cor_r * norm, -cor_i * norm
+
+
+def product_kernel(place, sign, mine, other, phase_turn, product, sums_out):
+    half, pixels = mine.shape[1], mine.shape[2]
+    block = 64
 
     def step(i, sums):
-        rows = pl.ds(pl.multiple_of(i * BLOCK, BLOCK), BLOCK)
-        real, imag = rows_back(mixed.at[0], mixed.at[1], turned, turn, rows)
-        return product_part(real, imag, returned, phase_turn, product, rows, sums)
+        rows = pl.ds(pl.multiple_of(i * block, block), block)
+        at = pl.ds(pl.multiple_of(place[0] * half + i * block, block), block)
+        turned_i = sign[0] * (other[0, rows, :] * mine[1, rows, :] - other[1, rows, :] * mine[0, rows, :])
+        pro_r = other[0, rows, :] * mine[0, rows, :] + other[1, rows, :] * mine[1, rows, :]
+        product[0, rows, :] = pro_r
+        product[1, rows, :] = turned_i
+        return add_sums(sums, pro_r, turned_i, phase_turn[0, at, :], phase_turn[1, at, :])
 
     zero = jnp.zeros((8, pixels), jnp.float32)
-    sums = lax.fori_loop(0, pixels // BLOCK, step, (zero, zero, zero))
-    weight_r, weight_i = weight_of(sums, pixels)
-    weight_r, weight_i = weight_r * flag[0], weight_i * flag[0]
-
-    def apply(i, carry):
-        rows = pl.ds(pl.multiple_of(i * 32, 32), 32)
-        pro_r, pro_i = product[0, rows, :], product[1, rows, :]
-        out[0, rows, :] = weight_r * pro_r - weight_i * pro_i
-        out[1, rows, :] = weight_r * pro_i + weight_i * pro_r
-        return carry
-
-    lax.fori_loop(0, pixels // 32, apply, 0)
+    sums = lax.fori_loop(0, half // block, step, (zero, zero, zero))
+    for i, value in enumerate(totals(sums, pixels)):
+        sums_out[i] = jnp.broadcast_to(value, sums_out.shape[1:])
 
 
 def final_kernel(
-    place, own, other, even, returned, phase_turn, drive,
+    place, own, other, even, returned, phase_turn, shared, sums_here, sums_there,
     matrix, turned, turn, turn_in, turn_out, cos_part, sin_part, sent_r, sent_i, far_r, far_i, mixed, product, kept_r, kept_i, sems,
 ):
     pixels = returned.shape[1]
@@ -413,25 +429,36 @@
         own, other, matrix, turned, turn_in, turn_out, cos_part, sin_part, 1, mixed
     )
 
-    def step(i, sums):
-        rows = pl.ds(pl.multiple_of(i * WIDE, WIDE), WIDE)
+    zero = jnp.zeros((8, pixels), jnp.float32)
+    sums = (zero, zero, zero)
+    for i in range(pixels // WIDE):
+        rows = pl.ds(i * WIDE, WIDE)
         real, imag = even_and_odd(even, mixed, turned, turn, rows)
-        return product_part(real, imag, returned, phase_turn, product, rows, sums)
-
-    zero = jnp.zeros((8, pixels), jnp.float32)
-    sums = lax.fori_loop(0, pixels // WIDE, step, (zero, zero, zero))
-    weight_r, weight_i = weight_of(sums, pixels)
+        sums = product_part(real, imag, returned, phase_turn, product, rows, sums)
+    weight_r, weight_i = weight_of(*totals(sums, pixels))
+    shared_r, shared_i = weight_of(
+        *(sums_here[i, 0:1, 0:1] + sums_there[i, 0:1, 0:1] for i in range(3))
+    )
     part = pixels // 4
 
     for out_r, out_i, core in ((kept_r, kept_i, place[0]), (sent_r, sent_i, 1 - place[0])):
         for s in range(2):
 
-            def apply(i, carry, s=s, out_r=out_r, out_i=out_i, core=core):
+            here = jnp.where(place[0] == s, 1.0, 0.0)
+            other_r, other_i = shared_r * here, shared_i * here
+
+            def apply(i, carry, s=s, out_r=out_r, out_i=out_i, core=core, other_r=other_r, other_i=other_i):
                 rows = pl.ds(pl.multiple_of((2 * s + core) * part + i * 32, 32), 32)
+                at = pl.ds(pl.multiple_of(core * part + i * 32, 32), 32)
                 to = pl.ds(pl.multiple_of(i * 32, 32), 32)
                 pro_r, pro_i = product[0, rows, :], product[1, rows, :]
-                out_r[s, to, :] = drive[0, rows, :] + (weight_r * pro_r - weight_i * pro_i)
-                out_i[s, to, :] = drive[1, rows, :] + (weight_r * pro_i + weight_i * pro_r)
+                sha_r, sha_i = shared[0, at, :], shared[1, at, :]
+                out_r[s, to, :] = (weight_r * pro_r - weight_i * pro_i) + (
+                    other_r * sha_r - other_i * sha_i
+                )
+                out_i[s, to, :] = (weight_r * pro_i + weight_i * pro_r) + (
+                    other_r * sha_i + other_i * sha_r
+                )
                 return carry
 
             lax.fori_loop(0, part // 32, apply, 0)
@@ -553,29 +580,41 @@
       tables["turn_out"], tables["cos_even"], tables["sin_even"])
 
 
-def last_call(flag, own, other, returned, phase_turn, tables):
+def shared_call(place, sign, own, other, tables):
     half = own.shape[2]
+    part = jax.ShapeDtypeStruct((2, half, 2 * half), jnp.float32)
     return pl.pallas_call(
-        last_kernel,
-        out_shape=jax.ShapeDtypeStruct(returned.shape, jnp.float32),
-        in_specs=[in_smem()] + in_vmem(13),
-        out_specs=in_vmem(1)[0],
-        scratch_shapes=[
-            pltpu.VMEM((2, 2, 2 * half, half), jnp.float32),
-            pltpu.VMEM(returned.shape, jnp.float32),
-        ],
+        shared_kernel,
+        out_shape=(part, part),
+        in_specs=[in_smem()] * 2 + in_vmem(11),
+        out_specs=tuple(in_vmem(2)),
+        scratch_shapes=[pltpu.VMEM((2, 2, 2 * half, half), jnp.float32)],
         compiler_params=limit(FIELD_LIMIT),
-        name="last",
-    )(flag.reshape(1), own, other, returned, phase_turn, *field_tables(tables))
-
-
-def final_call(place, own, other, even, returned, phase_turn, drive, tables):
+        name="shared",
+    )(place.reshape(1), sign.reshape(1), own, other, *field_tables(tables))
+
+
+def product_call(place, sign, mine, other, phase_turn):
+    return pl.pallas_call(
+        product_kernel,
+        out_shape=(
+            jax.ShapeDtypeStruct(mine.shape, jnp.float32),
+            jax.ShapeDtypeStruct((3, 8, 128), jnp.float32),
+        ),
+        in_specs=[in_smem()] * 2 + in_vmem(3),
+        out_specs=tuple(in_vmem(2)),
+        compiler_params=limit(ROWS_LIMIT),
+        name="product",
+    )(place.reshape(1), sign.reshape(1), mine, other, phase_turn)
+
+
+def final_call(place, own, other, even, returned, phase_turn, shared, sums_here, sums_there, tables):
     pixels = returned.shape[1]
     part = jax.ShapeDtypeStruct((2, pixels // 4, pixels), jnp.float32)
     return pl.pallas_call(
         final_kernel,
         out_shape=(part,) * 2 + (pltpu.HBM(part.shape, part.dtype),) * 2,
-        in_specs=[in_smem()] + in_vmem(13),
+        in_specs=[in_smem()] + in_vmem(15),
         out_specs=tuple(in_vmem(2)) + (pl.BlockSpec(memory_space=pltpu.HBM),) * 2,
         scratch_shapes=[
             pltpu.VMEM(even.shape, jnp.float32),
@@ -586,7 +625,7 @@
         ],
         compiler_params=limit(FINAL_LIMIT),
         name="final",
-    )(place.reshape(1), own, other, even, returned, phase_turn, drive, tables["matrix"], tables["turned"],
+    )(place.reshape(1), own, other, even, returned, phase_turn, shared, sums_here, sums_there, tables["matrix"], tables["turned"],
       tables["turn"], tables["turn_in"], tables["turn_out"], tables["cos_odd"], tables["sin_odd"])
 
 
@@ -656,7 +695,6 @@
     to_core = [(flat(m, s), flat(m ^ 1, s)) for m, s in everyone]
     to_x = [(flat(m, s), flat(m ^ 2, s)) for m, s in everyone]
     to_z = {j: [(flat(m, s), flat(m ^ (4 * j), s)) for m, s in everyone] for j in range(1, outer)}
-    last_mode = [(flat(m, 1 - m % 2), flat(m, m % 2)) for m in range(mode_size)]
 
     def send(value, pairs):
         return lax.ppermute(value, axes, pairs)
@@ -682,32 +720,35 @@
 
     last = jnp.full((), modes_here - 1, jnp.int32)
     both_fields = (backward_fields, forward_fields)
-    (rows_last_backward,) = rows_call(
-        last.reshape(1), (backward_fields,), ((0, True),), matrix, turn, True
-    )
-    got_last_backward = send(rows_last_backward, last_mode)
+    (sent_backward,) = rows_call(
+        (1 - space_index).reshape(1), (backward_fields,), ((0, True),), matrix, turn, True
+    )
+    got_backward = send(sent_backward, to_space)
     quarter = half // 4
     part = lax.dynamic_slice_in_dim(
-        phase, after(core_index * 2 + x_index, rows_last_backward) * quarter, quarter, axis=0
+        phase, after(core_index * 2 + x_index, sent_backward) * quarter, quarter, axis=0
     )
     other_part = send(part, to_space)
-    (rows_last_forward,) = rows_call(
-        after(last, part).reshape(1), (forward_fields,), ((0, True),), matrix, turn
-    )
-    got_last_forward = send(rows_last_forward, last_mode)
+    last_backward, last_forward = rows_call(
+        after(jnp.stack([last, last]), part), both_fields, ((0, True), (1, True)), matrix, turn
+    )
+    core_backward = send(last_backward, to_core)
+    modes = jnp.stack([1 - space_index])
+    sent_even, sent_odd = rows_call(
+        after(modes, last_backward), (forward_fields,), ((0, False),), matrix, turn
+    )
+    stays = core_index == space_index
+    sent_shared = jnp.where(stays, core_backward, last_forward)
+    got_shared = send(sent_shared, to_space)
+    own_shared = jnp.where(stays, last_forward, core_backward)
+    got_even = send(sent_even, to_space)
+    got_odd = send(sent_odd, to_space)
     cos_even, sin_even = permuted_transfer(pixels, 0)
     cos_odd, sin_odd = permuted_transfer(pixels, 1)
-    modes = jnp.stack([1 - space_index, 1 - space_index])
-    sent_backward, sent_even, sent_odd = rows_call(
-        after(modes, rows_last_forward), both_fields, ((0, True), (1, False)), matrix, turn
-    )
     modes = jnp.stack([space_index, space_index])
     own_backward, own_even, own_odd = rows_call(
-        after(modes, sent_odd), both_fields, ((0, True), (1, False)), matrix, turn
-    )
-    got_backward = send(sent_backward, to_space)
-    got_even = send(sent_even, to_space)
-    got_odd = send(sent_odd, to_space)
+        after(modes, sent_odd, sent_shared), both_fields, ((0, True), (1, False)), matrix, turn
+    )
 
     other_part = after(other_part, own_odd)
     other_phase = share(share(other_part, x_index, to_x), core_index, to_core)
@@ -729,39 +770,43 @@
         "sin_odd": sin_odd,
     }
 
-    takes_last = jnp.where(space_index == core_index, 1.0, 0.0)
-    returned = back_call(rows_last_backward, got_last_backward, tables)
-    drive = last_call(
-        takes_last, after(rows_last_forward, returned), got_last_forward, returned, phase_turn, tables
-    )
-    returned = back_call(after(own_backward, drive), got_backward, tables)
-    even = even_call(after(own_even, returned), got_even, tables)
+    sign = jnp.where(stays, 1.0, -1.0)
+    returned = back_call(own_backward, got_backward, tables)
+    give, mine = shared_call(core_index, sign, after(own_shared, returned), got_shared, tables)
+    shared, sums_here = product_call(core_index, sign, mine, send(give, to_core), phase_turn)
+    sums_there = send(sums_here, to_core)
+    even = even_call(after(own_even, sums_here), got_even, tables)
     sent_r, sent_i, kept_r, kept_i = final_call(
-        core_index, own_odd, got_odd, even, returned, phase_turn, drive, tables
+        core_index, own_odd, got_odd, even, returned, phase_turn, shared, sums_here, sums_there, tables
     )
     shape = (2, 2, outer, piece_rows, pixels)
-    real = (kept_r + send(sent_r, to_core)).reshape(shape)
-    imag = (kept_i + send(sent_i, to_core)).reshape(shape)
 
     def keep(value, axis, index):
         return lax.dynamic_index_in_dim(value, index, axis=axis, keepdims=False)
 
+    def core_step(kept, sent, axis, index, pairs):
+        kept, got = kept.reshape(shape), send(sent, to_core).reshape(shape)
+        leaves = keep(kept, axis, 1 - index) + keep(got, axis, 1 - index)
+        return keep(kept, axis, index) + keep(got, axis, index) + send(leaves, pairs)
+
     def step(value, axis, index, pairs):
         return keep(value, axis, index) + send(keep(value, axis, 1 - index), pairs)
 
-    real = step(real, 1, x_index, to_x)
-    imag = step(imag, 0, space_index, to_space)
+    real = core_step(kept_r, sent_r, 1, x_index, to_x)
+    imag = core_step(kept_i, sent_i, 0, space_index, to_space)
     real = step(real, 0, space_index, to_space)
     imag = step(imag, 0, x_index, to_x)
     both = by_z(jnp.stack([real, imag], axis=1))
+    got = {j: send(both[j], to_z[j]) for j in range(1, outer)}
     total = both[0]
     for j in range(1, outer):
-        total = total + send(both[j], to_z[j])
+        total = total + got[j]
     mode_root = math.sqrt(modes_here * mode_size)
     place = (core_index * 2 + x_index) * outer + z_index
     piece = lax.dynamic_slice_in_dim(phase, place * piece_rows, piece_rows, axis=0)
     updated = phase_update(total[0] / mode_root, total[1] / mode_root, piece)
-    pieces = by_z(jnp.stack([updated] + [send(updated, to_z[j]) for j in range(1, outer)]))
+    got = {j: send(updated, to_z[j]) for j in range(1, outer)}
+    pieces = by_z(jnp.stack([updated] + [got[j] for j in range(1, outer)]))
     pieces = share(share(pieces, x_index, to_x), core_index, to_core)
     return pieces.reshape(half, pixels)
 

time: 144 us -> 146 us (1.014)
  Pallas kernels: 51.4 us -> 42.9 us
  other arithmetic: 10.9 us -> 16.6 us
  waiting for transfers between devices: 49.6 us -> 53.4 us
  local copies, waits for them, and re-layouts: 3.04 us -> 4.87 us
    pallas_call x2 -> x1, Pallas kernels: 14.7 us -> 8.02 us  [back_call(): pl.pallas_call(back_kernel, out_shape=jax.ShapeDtypeStruct((2, 2 * half,...]
    ppermute x22 -> x24, waiting for transfers between devices: 49.6 us -> 53.4 us  [send(): return lax.ppermute(value, axes, pairs)]
    select_n x0 -> x1, other arithmetic: none -> 2.83 us  [whole_modes(): own_shared = jnp.where(stays, last_forward, core_backward)]
    unnamed x26 -> x34, local copies, waits for them, and re-layouts: 1.77 us -> 3.66 us
    add x3 -> x5, other arithmetic: 1.22 us -> 3.1 us  [the longest x2 2 us: core_step(): leaves = keep(kept, axis, 1 - index) + keep(got, axis, 1 - index)]
    pallas_call x1 -> x2, Pallas kernels: 9.21 us -> 8.44 us  [the longest x1 7.85 us: shared_call(): pl.pallas_call(shared_kernel, out_shape=(part, part), in_specs=[in_smem()...]
    ppermute x22 -> x24, starting transfers between devices: 27.6 us -> 27.1 us  [send(): return lax.ppermute(value, axes, pairs)]
  transfers between devices with their start and end apart: 22 -> 24, of which waited for: 16 -> 16; matrix products, arithmetic and copies ran while one was open for 7% -> 11% of each run, Pallas kernels for 28% -> 23%
where the time goes in v1:
time: 146 us; the launch traced here: 145 us
  waiting for transfers between devices  53.4 us (37%)
  Pallas kernels  42.9 us (29%)
  starting transfers between devices  27.1 us (19%)
  other arithmetic  16.6 us (11%)
  local copies, waits for them, and re-layouts  4.87 us (3%)
    ppermute x24, waiting for transfers between devices, send(): return lax.ppermute(value, axes, pairs)  53.4 us
    ppermute x24, starting transfers between devices, send(): return lax.ppermute(value, axes, pairs)  27.1 us
    pallas_call x4, Pallas kernels, rows_call(): pl.pallas_call(kernel, out_shape=tuple(shapes), in_specs=[in_smem()] + [p...  15.7 us
    pallas_call x1, Pallas kernels, back_call(): pl.pallas_call(back_kernel, out_shape=jax.ShapeDtypeStruct((2, 2 * half,...  8.02 us
    pallas_call x1, Pallas kernels, shared_call(): pl.pallas_call(shared_kernel, out_shape=(part, part), in_specs=[in_smem()...  7.85 us
    pallas_call x1, Pallas kernels, final_call(): pl.pallas_call(final_kernel, out_shape=(part,) * 2 + (pltpu.HBM(part.shap...  6.46 us
    pallas_call x1, Pallas kernels, even_call(): pl.pallas_call(even_kernel, out_shape=jax.ShapeDtypeStruct((2, 2 * half,...  4.34 us
    unnamed x34, local copies, waits for them, and re-layouts  3.66 us
  transfers between devices with their start and end apart: 24, of which 16 were waited for; matrix products, arithmetic and copies ran while one was open for 11% of the time, Pallas kernels for 23%

profile of v1, /device:TPU:0, one launch (start us, length us, event | category | flops | bytes accessed | tf_op | source)
XLA Modules:
  0.0 145.5 jit_solution(18283718489330359142)
XLA Ops:
  0.0 3.7 %rows.4 = f32[2,2,256,256]{3,2,1,0:T(8,128)} custom-call(s32[1]{0:T(128)} %bitcast.2.index, f32[2,3,256,512]{3,2,1,0:T(8,128)} %refs_0_.7, bf16[2,512,512]{2,1,0:T(8,128)(2,1)} %constant.207.clone.refs_1_.refs_2_.matrix, f32[2,256]{1,0:T(2,128)} %constant.208.clone.refs_2_.refs_3_.turn), custom_call_target="tpu_custom_call" | custom-call | tf_op jit(solution)/shard_map/rows/pallas_call | solution.py:540
  3.7 3.1 %collective-permute-start.2 = (f32[2,2,256,256]{3,2,1,0:T(8,128)}, f32[2,2,256,256]{3,2,1,0:T(8,128)}, u32[]{:S(2)}, u32[]{:S(2)}) collective-permute-start(f32[2,2,256,256]{3,2,1,0:T(8,128)} %rows.4), channel_id=1, source_target_pairs={{0,1},{1,0},{2,3},{3,2},{4,5},{5,4},{6,7},{7,6},{8,9},{9,8},{10,11... | collective-permute-start | bytes 3145736 | tf_op jit(solution)/shard_map/ppermute | solution.py:700
  6.8 0.9 constant_dynamic-slice_fusion
  7.9 4.7 %rows.5 = (f32[2,2,256,256]{3,2,1,0:T(8,128)}, f32[2,2,256,256]{3,2,1,0:T(8,128)S(1)}) custom-call(s32[2]{0:T(128)S(1)} %broadcast.336.index, f32[2,3,256,512]{3,2,1,0:T(8,128)} %refs_0_.7, f32[2,3,256,512]{3,2,1,0:T(8,128)} %refs_1_.5, bf16[2,512,512]{2,1,0:T(8,128)(2,1)S(1)} %copy-done, f32[2,256]{1,0:T(2,128)S(1)} %copy-done.12), custom_call_target="tpu_custom_call" | custom-call | tf_op jit(solution)/shard_map/rows/pallas_call | solution.py:540
  12.7 3.3 %rows.6 = (f32[2,256,256]{2,1,0:T(8,128)}, f32[2,256,256]{2,1,0:T(8,128)}) custom-call(s32[1]{0:T(128)} %bitcast.2.index, f32[2,3,256,512]{3,2,1,0:T(8,128)} %refs_1_.5, bf16[2,512,512]{2,1,0:T(8,128)(2,1)S(1)} %copy-done, f32[2,256]{1,0:T(2,128)S(1)} %copy-done.12), custom_call_target="tpu_custom_call" | custom-call | tf_op jit(solution)/shard_map/rows/pallas_call | solution.py:540
  15.9 2.0 %collective-permute-start.8 = (f32[2,256,256]{2,1,0:T(8,128)}, f32[2,256,256]{2,1,0:T(8,128)}, u32[]{:S(2)}, u32[]{:S(2)}) collective-permute-start(f32[2,256,256]{2,1,0:T(8,128)} %get-tuple-element.43), channel_id=1, source_target_pairs={{0,1},{1,0},{2,3},{3,2},{4,5},{5,4},{6,7},{7,6},{8,9},{9,8},{10,11... | collective-permute-start | bytes 1572872 | tf_op jit(solution)/shard_map/ppermute | solution.py:700
  18.9 1.1 maximum_bitcast_fusion
  20.0 2.9 %fusion.20 = (f32[2,256,256]{2,1,0:T(8,128)}, f32[2,256,256]{2,1,0:T(8,128)}, f32[2,256,256]{2,1,0:T(8,128)S(1)}, f32[2,256,256]{2,1,0:T(8,128)S(1)}) fusion(f32[256]{0:T(256)S(1)} %bitcast.136, f32[2,256]{1,0:T(2,128)S(1)} %fusion.43, f32[256]{0:T(256)S(1)} %bitcast.137), kind=kLoop, calls=%fused_computation.52 | loop fusion | flops 12058624 | bytes 2101248 | tf_op jit(solution)/shard_map/div | solution.py:670
  22.9 2.8 %broadcast_select_fusion = (f32[2,2,256,256]{3,2,1,0:T(8,128)}, f32[2,2,256,256]{3,2,1,0:T(8,128)}) fusion(f32[2,2,256,256]{3,2,1,0:T(8,128)S(1)} %get-tuple-element.32, f32[2,2,256,256]{3,2,1,0:T(8,128)} %collective-permute-done, pred[]{:T(512)S(6)} %eq.140), kind=kLoop, calls=%fused_computation.75 | loop fusion | flops 524288 | bytes 4194305 | tf_op jit(solution)/shard_map/jit(_where)/select_n | solution.py:743
  25.7 1.9 %collective-permute-start.3 = (f32[2,2,256,256]{3,2,1,0:T(8,128)}, f32[2,2,256,256]{3,2,1,0:T(8,128)}, u32[]{:S(2)}, u32[]{:S(2)}) collective-permute-start(f32[2,2,256,256]{3,2,1,0:T(8,128)} %get-tuple-element.50), channel_id=1, source_target_pairs={{0,1},{1,0},{2,3},{3,2},{4,5},{5,4},{6,7},{7,6},{8,9},{9,8},{10,11... | collective-permute-start | bytes 3145736 | tf_op jit(solution)/shard_map/ppermute | solution.py:700
  27.7 4.0 %rows.7 = (f32[2,2,256,256]{3,2,1,0:T(8,128)S(1)}, f32[2,256,256]{2,1,0:T(8,128)S(1)}, f32[2,256,256]{2,1,0:T(8,128)S(1)}) custom-call(s32[2]{0:T(128)S(1)} %pad_add_fusion.index, f32[2,3,256,512]{3,2,1,0:T(8,128)} %refs_0_.7, f32[2,3,256,512]{3,2,1,0:T(8,128)} %refs_1_.5, bf16[2,512,512]{2,1,0:T(8,128)(2,1)S(1)} %copy-done, f32[2,256]{1,0:T(2,128)S(1)} %copy-done.12), custom_call_target="tpu_custom_call" | custom-call | tf_op jit(solution)/shard_map/rows/pallas_call | solution.py:540
  31.7 2.1 %collective-permute-done.5 = f32[64,512]{1,0:T(8,128)S(1)} collective-permute-done((f32[64,512]{1,0:T(8,128)S(1)}, f32[64,512]{1,0:T(8,128)S(1)}, u32[]{:S(2)}, u32[]{:S(2)}) %collective-permute-start.5) | collective-permute-done | bytes 131104 | tf_op jit(solution)/shard_map/ppermute | solution.py:700
  33.8 2.0 %collective-permute-start.6 = (f32[64,512]{1,0:T(8,128)S(1)}, f32[64,512]{1,0:T(8,128)S(1)}, u32[]{:S(2)}, u32[]{:S(2)}) collective-permute-start(f32[64,512]{1,0:T(8,128)S(1)} %collective-permute-done.5), channel_id=1, source_target_pairs={{0,4},{1,5},{2,6},{3,7},{4,0},{5,1},{6,2},{7,3},{8,12},{9,13},{10,... | collective-permute-start | bytes 393224 | tf_op jit(solution)/shard_map/ppermute | solution.py:700
  36.0 2.8 %collective-permute-done.6 = f32[64,512]{1,0:T(8,128)S(1)} collective-permute-done((f32[64,512]{1,0:T(8,128)S(1)}, f32[64,512]{1,0:T(8,128)S(1)}, u32[]{:S(2)}, u32[]{:S(2)}) %collective-permute-start.6) | collective-permute-done | bytes 131104 | tf_op jit(solution)/shard_map/ppermute | solution.py:700
  40.0 1.0 copy-done.1
  41.0 1.0 copy-done.3
  42.1 1.2 copy-done.7
  43.3 8.0 %back.1.returned = f32[2,512,512]{2,1,0:T(8,128)S(1)} custom-call(f32[2,2,256,256]{3,2,1,0:T(8,128)S(1)} %copy-done.7, f32[2,2,256,256]{3,2,1,0:T(8,128)} %collective-permute-done.2.other, bf16[2,512,512]{2,1,0:T(8,128)(2,1)S(1)} %copy-done, bf16[2,512,512]{2,1,0:T(8,128)(2,1)S(1)} %pad_maximum_fusion.2.turned, f32[2,256]{1,0:T(2,128)S(1)} %copy-done.12, ...), custom_call_target="tpu_custom_call" | custom-call | tf_op jit(solution)/shard_map/back/pallas_call | solution.py:558
  51.4 1.1 pad_maximum_fusion.4
  52.5 25.6 %collective-permute-done.3.other = f32[2,2,256,256]{3,2,1,0:T(8,128)} collective-permute-done((f32[2,2,256,256]{3,2,1,0:T(8,128)}, f32[2,2,256,256]{3,2,1,0:T(8,128)}, u32[]{:S(2)}, u32[]{:S(2)}) %collective-permute-start.3) | collective-permute-done | bytes 1048608 | tf_op jit(solution)/shard_map/ppermute | solution.py:700
  78.0 7.8 %shared.1 = (f32[2,256,512]{2,1,0:T(8,128)S(1)}, f32[2,256,512]{2,1,0:T(8,128)S(1)}) custom-call(s32[1]{0:T(128)} %bitcast.place, f32[1]{0:T(128)} %bitcast.3.sign, f32[2,2,256,256]{3,2,1,0:T(8,128)S(1)} %copy-done.5, f32[2,2,256,256]{3,2,1,0:T(8,128)} %collective-permute-done.3.other, bf16[2,512,512]{2,1,0:T(8,128)(2,1)S(1)} %copy-done, ...), custom_call_target="tpu_custom_call" | custom-call | tf_op jit(solution)/shard_map/shared/pallas_call | solution.py:586
  86.2 1.3 negate_select_fusion.1
  87.7 0.9 collective-permute-done.4.other
  89.6 4.3 %even.1 = f32[2,512,256]{2,1,0:T(8,128)S(1)} custom-call(f32[2,256,256]{2,1,0:T(8,128)S(1)} %copy-done.9, f32[2,256,256]{2,1,0:T(8,128)} %collective-permute-done.8.other, bf16[2,512,512]{2,1,0:T(8,128)(2,1)S(1)} %copy-done, bf16[2,512,512]{2,1,0:T(8,128)(2,1)S(1)} %pad_maximum_fusion.2.turned, f32[2,256,128]{2,1,0:T(8,128)S(1)} %broadcast_in_dim.4.turn_in, ...), custom_call_target="tpu_custom_call" | custom-call | tf_op jit(solution)/shard_map/even/pallas_call | solution.py:571
  94.0 6.5 %final.1 = (f32[2,128,512]{2,1,0:T(8,128)S(1)}, f32[2,128,512]{2,1,0:T(8,128)S(1)}, f32[2,128,512]{2,1,0:T(8,128)}, f32[2,128,512]{2,1,0:T(8,128)}) custom-call(s32[1]{0:T(128)} %bitcast.place, f32[2,256,256]{2,1,0:T(8,128)S(1)} %copy-done.11, f32[2,256,256]{2,1,0:T(8,128)} %collective-permute-done.1.other, f32[2,512,256]{2,1,0:T(8,128)S(1)} %even.1, ...), custom_call_target="tpu_custom_call" | custom-call | tf_op jit(solution)/shard_map/final/pallas_call | solution.py:614
  101.1 1.4 collective-permute-done.10
  102.5 1.0 add_bitcast_fusion.1
  103.5 1.8 %collective-permute-start.11 = (f32[2,4,16,512]{3,2,1,0:T(8,128)S(1)}, f32[2,4,16,512]{3,2,1,0:T(8,128)S(1)}, u32[]{:S(2)}, u32[]{:S(2)}) collective-permute-start(f32[2,4,16,512]{3,2,1,0:T(8,128)S(1)} %add_bitcast_fusion.1), channel_id=1, source_target_pairs={{0,4},{1,5},{2,6},{3,7},{4,0},{5,1},{6,2},{7,3},{8,12},{9,13},{10,... | collective-permute-start | bytes 786440 | tf_op jit(solution)/shard_map/ppermute | solution.py:700
  105.3 1.0 add_bitcast_fusion
  106.3 1.6 %collective-permute-start.14 = (f32[2,4,16,512]{3,2,1,0:T(8,128)S(1)}, f32[2,4,16,512]{3,2,1,0:T(8,128)S(1)}, u32[]{:S(2)}, u32[]{:S(2)}) collective-permute-start(f32[2,4,16,512]{3,2,1,0:T(8,128)S(1)} %add_bitcast_fusion), channel_id=1, source_target_pairs={{0,1},{1,0},{2,3},{3,2},{4,5},{5,4},{6,7},{7,6},{8,9},{9,8},{10,11... | collective-permute-start | bytes 786440 | tf_op jit(solution)/shard_map/ppermute | solution.py:700
  107.9 4.1 %collective-permute-done.11 = f32[2,4,16,512]{3,2,1,0:T(8,128)S(1)} collective-permute-done((f32[2,4,16,512]{3,2,1,0:T(8,128)S(1)}, f32[2,4,16,512]{3,2,1,0:T(8,128)S(1)}, u32[]{:S(2)}, u32[]{:S(2)}) %collective-permute-start.11) | collective-permute-done | bytes 262176 | tf_op jit(solution)/shard_map/ppermute | solution.py:700
  111.9 1.0 fusion.30
  113.0 1.8 %collective-permute-start.12 = (f32[4,16,512]{2,1,0:T(8,128)S(1)}, f32[4,16,512]{2,1,0:T(8,128)S(1)}, u32[]{:S(2)}, u32[]{:S(2)}) collective-permute-start(f32[4,16,512]{2,1,0:T(8,128)S(1)} %dynamic-slice_bitcast_fusion.1), channel_id=1, source_target_pairs={{0,1},{1,0},{2,3},{3,2},{4,5},{5,4},{6,7},{7,6},{8,9},{9,8},{10,11... | collective-permute-start | bytes 393224 | tf_op jit(solution)/shard_map/ppermute | solution.py:700
  114.9 1.5 %collective-permute-start.15 = (f32[4,16,512]{2,1,0:T(8,128)S(1)}, f32[4,16,512]{2,1,0:T(8,128)S(1)}, u32[]{:S(2)}, u32[]{:S(2)}) collective-permute-start(f32[4,16,512]{2,1,0:T(8,128)S(1)} %dynamic-slice_bitcast_fusion), channel_id=1, source_target_pairs={{0,4},{1,5},{2,6},{3,7},{4,0},{5,1},{6,2},{7,3},{8,12},{9,13},{10,... | collective-permute-start | bytes 393224 | tf_op jit(solution)/shard_map/ppermute | solution.py:700
  116.4 1.6 %collective-permute-done.12 = f32[4,16,512]{2,1,0:T(8,128)S(1)} collective-permute-done((f32[4,16,512]{2,1,0:T(8,128)S(1)}, f32[4,16,512]{2,1,0:T(8,128)S(1)}, u32[]{:S(2)}, u32[]{:S(2)}) %collective-permute-start.12) | collective-permute-done | bytes 131104 | tf_op jit(solution)/shard_map/ppermute | solution.py:700
  118.0 1.9 %collective-permute-done.15 = f32[4,16,512]{2,1,0:T(8,128)S(1)} collective-permute-done((f32[4,16,512]{2,1,0:T(8,128)S(1)}, f32[4,16,512]{2,1,0:T(8,128)S(1)}, u32[]{:S(2)}, u32[]{:S(2)}) %collective-permute-start.15) | collective-permute-done | bytes 131104 | tf_op jit(solution)/shard_map/ppermute | solution.py:700
  120.0 1.6 %collective-permute-start.16 = (f32[2,16,512]{2,1,0:T(8,128)S(1)}, f32[2,16,512]{2,1,0:T(8,128)S(1)}, u32[]{:S(2)}, u32[]{:S(2)}) collective-permute-start(f32[2,16,512]{2,1,0:T(8,128)S(1)} %get-tuple-element.55), channel_id=1, source_target_pairs={{0,8},{1,9},{2,10},{3,11},{4,12},{5,13},{6,14},{7,15},{8,0},{9,1},... | collective-permute-start | bytes 196616 | tf_op jit(solution)/shard_map/ppermute | solution.py:700
  121.7 2.5 %collective-permute-start.18 = (f32[2,16,512]{2,1,0:T(8,128)S(1)}, f32[2,16,512]{2,1,0:T(8,128)S(1)}, u32[]{:S(2)}, u32[]{:S(2)}) collective-permute-start(f32[2,16,512]{2,1,0:T(8,128)S(1)} %get-tuple-element.56), channel_id=1, source_target_pairs={{0,24},{1,25},{2,26},{3,27},{4,28},{5,29},{6,30},{7,31},{8,16},{9,... | collective-permute-start | bytes 196616 | tf_op jit(solution)/shard_map/ppermute | solution.py:700
  125.1 2.8 %collective-permute-done.18 = f32[2,16,512]{2,1,0:T(8,128)S(1)} collective-permute-done((f32[2,16,512]{2,1,0:T(8,128)S(1)}, f32[2,16,512]{2,1,0:T(8,128)S(1)}, u32[]{:S(2)}, u32[]{:S(2)}) %collective-permute-start.18) | collective-permute-done | bytes 65568 | tf_op jit(solution)/shard_map/ppermute | solution.py:700
  127.8 2.4 %collective-permute-done.17 = f32[2,16,512]{2,1,0:T(8,128)S(1)} collective-permute-done((f32[2,16,512]{2,1,0:T(8,128)S(1)}, f32[2,16,512]{2,1,0:T(8,128)S(1)}, u32[]{:S(2)}, u32[]{:S(2)}) %collective-permute-start.17) | collective-permute-done | bytes 65568 | tf_op jit(solution)/shard_map/ppermute | solution.py:700
  130.2 0.9 multiply_subtract_fusion
  131.1 1.5 %collective-permute-start.21 = (f32[16,512]{1,0:T(8,128)S(1)}, f32[16,512]{1,0:T(8,128)S(1)}, u32[]{:S(2)}, u32[]{:S(2)}) collective-permute-start(f32[16,512]{1,0:T(8,128)S(1)} %multiply_subtract_fusion), channel_id=1, source_target_pairs={{0,24},{1,25},{2,26},{3,27},{4,28},{5,29},{6,30},{7,31},{8,16},{9,... | collective-permute-start | bytes 98312 | tf_op jit(solution)/shard_map/ppermute | solution.py:700
  132.6 3.0 %collective-permute-start.19 = (f32[16,512]{1,0:T(8,128)S(1)}, f32[16,512]{1,0:T(8,128)S(1)}, u32[]{:S(2)}, u32[]{:S(2)}) collective-permute-start(f32[16,512]{1,0:T(8,128)S(1)} %multiply_subtract_fusion), channel_id=1, source_target_pairs={{0,8},{1,9},{2,10},{3,11},{4,12},{5,13},{6,14},{7,15},{8,0},{9,1},... | collective-permute-start | bytes 98312 | tf_op jit(solution)/shard_map/ppermute | solution.py:700
  135.6 1.3 collective-permute-done.21
  137.9 1.6 %collective-permute-start.22 = (f32[4,16,512]{2,1,0:T(8,128)S(1)}, f32[4,16,512]{2,1,0:T(8,128)S(1)}, u32[]{:S(2)}, u32[]{:S(2)}) collective-permute-start(f32[4,16,512]{2,1,0:T(8,128)S(1)} %bitcast.117), channel_id=1, source_target_pairs={{0,4},{1,5},{2,6},{3,7},{4,0},{5,1},{6,2},{7,3},{8,12},{9,13},{10,... | collective-permute-start | bytes 393224 | tf_op jit(solution)/shard_map/ppermute | solution.py:700
  139.5 3.5 %collective-permute-done.22 = f32[4,16,512]{2,1,0:T(8,128)S(1)} collective-permute-done((f32[4,16,512]{2,1,0:T(8,128)S(1)}, f32[4,16,512]{2,1,0:T(8,128)S(1)}, u32[]{:S(2)}, u32[]{:S(2)}) %collective-permute-start.22) | collective-permute-done | bytes 131104 | tf_op jit(solution)/shard_map/ppermute | solution.py:700
  143.1 1.5 %collective-permute-done.23 = f32[2,4,16,512]{3,2,1,0:T(8,128)S(1)} collective-permute-done((f32[2,4,16,512]{3,2,1,0:T(8,128)S(1)}, f32[2,4,16,512]{3,2,1,0:T(8,128)S(1)}, u32[]{:S(2)}, u32[]{:S(2)}) %collective-permute-start.23) | collective-permute-done | bytes 262176 | tf_op jit(solution)/shard_map/ppermute | solution.py:700
  144.6 0.8 reverse_select_fusion.1
  (91 shorter events, 7.0 us)
Async XLA Ops:
  0.0 7.8 %copy-start = (bf16[2,512,512]{2,1,0:T(8,128)(2,1)S(1)}, bf16[2,512,512]{2,1,0:T(8,128)(2,1)}, u32[]{:S(2)}) copy-start(bf16[2,512,512]{2,1,0:T(8,128)(2,1)} %constant.207.clone.refs_1_.refs_2_.matrix) | copy-start | bytes 3145732
  0.0 7.8 %copy-start.12 = (f32[2,256]{1,0:T(2,128)S(1)}, f32[2,256]{1,0:T(2,128)}, u32[]{:S(2)}) copy-start(f32[2,256]{1,0:T(2,128)} %constant.208.clone.refs_2_.refs_3_.turn) | copy-start | bytes 6148
  3.7 36.0 %collective-permute-start.2 = (f32[2,2,256,256]{3,2,1,0:T(8,128)}, f32[2,2,256,256]{3,2,1,0:T(8,128)}, u32[]{:S(2)}, u32[]{:S(2)}) collective-permute-start(f32[2,2,256,256]{3,2,1,0:T(8,128)} %rows.4), channel_id=1, source_target_pairs={{0,1},{1,0},{2,3},{3,2},{4,5},{5,4},{6,7},{7,6},{8,9},{9,8},{10,11... | collective-permute-start | bytes 3145736 | tf_op jit(solution)/shard_map/ppermute | solution.py:700
  7.7 26.1 %collective-permute-start.5 = (f32[64,512]{1,0:T(8,128)S(1)}, f32[64,512]{1,0:T(8,128)S(1)}, u32[]{:S(2)}, u32[]{:S(2)}) collective-permute-start(f32[64,512]{1,0:T(8,128)S(1)} %constant_dynamic-slice_fusion), channel_id=1, source_target_pairs={{0,1},{1,0},{2,3},{3,2},{4,5},{5,4},{6,7},{7,6},{8,9},{9,8},{10,11... | collective-permute-start | bytes 393224 | tf_op jit(solution)/shard_map/ppermute | solution.py:700
  12.6 10.3 %collective-permute-start = (f32[2,2,256,256]{3,2,1,0:T(8,128)}, f32[2,2,256,256]{3,2,1,0:T(8,128)}, u32[]{:S(2)}, u32[]{:S(2)}) collective-permute-start(f32[2,2,256,256]{3,2,1,0:T(8,128)} %get-tuple-element.29), channel_id=1, source_target_pairs={{0,2},{1,3},{2,0},{3,1},{4,6},{5,7},{6,4},{7,5},{8,10},{9,11},{10,... | collective-permute-start | bytes 3145736 | tf_op jit(solution)/shard_map/ppermute | solution.py:700
  15.9 73.4 %collective-permute-start.8 = (f32[2,256,256]{2,1,0:T(8,128)}, f32[2,256,256]{2,1,0:T(8,128)}, u32[]{:S(2)}, u32[]{:S(2)}) collective-permute-start(f32[2,256,256]{2,1,0:T(8,128)} %get-tuple-element.43), channel_id=1, source_target_pairs={{0,1},{1,0},{2,3},{3,2},{4,5},{5,4},{6,7},{7,6},{8,9},{9,8},{10,11... | collective-permute-start | bytes 1572872 | tf_op jit(solution)/shard_map/ppermute | solution.py:700
  17.9 76.0 %collective-permute-start.1 = (f32[2,256,256]{2,1,0:T(8,128)}, f32[2,256,256]{2,1,0:T(8,128)}, u32[]{:S(2)}, u32[]{:S(2)}) collective-permute-start(f32[2,256,256]{2,1,0:T(8,128)} %get-tuple-element.31), channel_id=1, source_target_pairs={{0,1},{1,0},{2,3},{3,2},{4,5},{5,4},{6,7},{7,6},{8,9},{9,8},{10,11... | collective-permute-start | bytes 1572872 | tf_op jit(solution)/shard_map/ppermute | solution.py:700
  25.7 52.3 %collective-permute-start.3 = (f32[2,2,256,256]{3,2,1,0:T(8,128)}, f32[2,2,256,256]{3,2,1,0:T(8,128)}, u32[]{:S(2)}, u32[]{:S(2)}) collective-permute-start(f32[2,2,256,256]{3,2,1,0:T(8,128)} %get-tuple-element.50), channel_id=1, source_target_pairs={{0,1},{1,0},{2,3},{3,2},{4,5},{5,4},{6,7},{7,6},{8,9},{9,8},{10,11... | collective-permute-start | bytes 3145736 | tf_op jit(solution)/shard_map/ppermute | solution.py:700
  27.7 8.1 %copy-start.13 = (f32[1,256,512]{2,1,0:T(8,128)S(1)}, f32[1,256,512]{2,1,0:T(8,128)}, u32[]{:S(2)}) copy-start(f32[1,256,512]{2,1,0:T(8,128)} %get-tuple-element.58) | copy-start | bytes 1572868
  27.7 8.1 %copy-start.14 = (f32[1,256,512]{2,1,0:T(8,128)S(1)}, f32[1,256,512]{2,1,0:T(8,128)}, u32[]{:S(2)}) copy-start(f32[1,256,512]{2,1,0:T(8,128)} %get-tuple-element.59) | copy-start | bytes 1572868
  31.7 7.8 %copy-start.6 = (f32[2,2,256,256]{3,2,1,0:T(8,128)}, f32[2,2,256,256]{3,2,1,0:T(8,128)S(1)}, u32[]{:S(2)}) copy-start(f32[2,2,256,256]{3,2,1,0:T(8,128)S(1)} %get-tuple-element.36.own) | copy-start | bytes 3145732
  31.7 7.8 %copy-start.8 = (f32[2,256,256]{2,1,0:T(8,128)}, f32[2,256,256]{2,1,0:T(8,128)S(1)}, u32[]{:S(2)}) copy-start(f32[2,256,256]{2,1,0:T(8,128)S(1)} %get-tuple-element.42.own) | copy-start | bytes 1572868
  31.7 7.8 %copy-start.10 = (f32[2,256,256]{2,1,0:T(8,128)}, f32[2,256,256]{2,1,0:T(8,128)S(1)}, u32[]{:S(2)}) copy-start(f32[2,256,256]{2,1,0:T(8,128)S(1)} %get-tuple-element.34.own) | copy-start | bytes 1572868
  33.8 5.0 %collective-permute-start.6 = (f32[64,512]{1,0:T(8,128)S(1)}, f32[64,512]{1,0:T(8,128)S(1)}, u32[]{:S(2)}, u32[]{:S(2)}) collective-permute-start(f32[64,512]{1,0:T(8,128)S(1)} %collective-permute-done.5), channel_id=1, source_target_pairs={{0,4},{1,5},{2,6},{3,7},{4,0},{5,1},{6,2},{7,3},{8,12},{9,13},{10,... | collective-permute-start | bytes 393224 | tf_op jit(solution)/shard_map/ppermute | solution.py:700
  39.6 11.8 %collective-permute-start.7 = (f32[2,64,512]{2,1,0:T(8,128)}, f32[2,64,512]{2,1,0:T(8,128)}, u32[]{:S(2)}, u32[]{:S(2)}) collective-permute-start(f32[2,64,512]{2,1,0:T(8,128)} %reverse_select_fusion.6), channel_id=1, source_target_pairs={{0,2},{1,3},{2,0},{3,1},{4,6},{5,7},{6,4},{7,5},{8,10},{9,11},{10,... | collective-permute-start | bytes 786440 | tf_op jit(solution)/shard_map/ppermute | solution.py:700
  40.0 1.0 copy-start.1
  41.0 1.0 copy-start.3
  42.1 1.2 copy-start.7
  51.3 26.7 %copy-start.5 = (f32[2,2,256,256]{3,2,1,0:T(8,128)S(1)}, f32[2,2,256,256]{3,2,1,0:T(8,128)}, u32[]{:S(2)}) copy-start(f32[2,2,256,256]{3,2,1,0:T(8,128)} %get-tuple-element.37.own) | copy-start | bytes 3145732
  78.0 8.0 %copy-start.15 = (f32[256,512]{1,0:T(8,128)S(1)}, f32[256,512]{1,0:T(8,128)}, u32[]{:S(2)}) copy-start(f32[256,512]{1,0:T(8,128)} %param.7) | copy-start | bytes 1572868
  85.9 2.7 %collective-permute-start.4 = (f32[2,256,512]{2,1,0:T(8,128)S(1)}, f32[2,256,512]{2,1,0:T(8,128)S(1)}, u32[]{:S(2)}, u32[]{:S(2)}) collective-permute-start(f32[2,256,512]{2,1,0:T(8,128)S(1)} %get-tuple-element.39), channel_id=1, source_target_pairs={{0,2},{1,3},{2,0},{3,1},{4,6},{5,7},{6,4},{7,5},{8,10},{9,11},{10,... | collective-permute-start | bytes 3145736 | tf_op jit(solution)/shard_map/ppermute | solution.py:700
  88.6 1.0 copy-start.9
  89.2 4.8 %collective-permute-start.9 = (f32[3,8,128]{2,1,0:T(8,128)S(1)}, f32[3,8,128]{2,1,0:T(8,128)S(1)}, u32[]{:S(2)}, u32[]{:S(2)}) collective-permute-start(f32[3,8,128]{2,1,0:T(8,128)S(1)} %get-tuple-element.41.sums_here), channel_id=1, source_target_pairs={{0,2},{1,3},{2,0},{3,1},{4,6},{5,7},{6,4},{7,5},{8,10},{9,11},{10,... | collective-permute-start | bytes 36872 | tf_op jit(solution)/shard_map/ppermute | solution.py:700
  89.3 4.7 %copy-start.2 = (f32[2,256,256]{2,1,0:T(8,128)S(1)}, f32[2,256,256]{2,1,0:T(8,128)}, u32[]{:S(2)}) copy-start(f32[2,256,256]{2,1,0:T(8,128)} %get-tuple-element.60.sin_odd.sin_part) | copy-start | bytes 1572868
  89.3 4.7 %copy-start.4 = (f32[2,256,256]{2,1,0:T(8,128)S(1)}, f32[2,256,256]{2,1,0:T(8,128)}, u32[]{:S(2)}) copy-start(f32[2,256,256]{2,1,0:T(8,128)} %get-tuple-element.61.cos_odd.cos_part) | copy-start | bytes 1572868
  89.3 4.7 %copy-start.11 = (f32[2,256,256]{2,1,0:T(8,128)S(1)}, f32[2,256,256]{2,1,0:T(8,128)}, u32[]{:S(2)}) copy-start(f32[2,256,256]{2,1,0:T(8,128)} %copy-done.10) | copy-start | bytes 1572868
  100.5 14.3 %copy-start.16 = (f32[2,128,512]{2,1,0:T(8,128)S(1)}, f32[2,128,512]{2,1,0:T(8,128)}, u32[]{:S(2)}) copy-start(f32[2,128,512]{2,1,0:T(8,128)} %get-tuple-element.47) | copy-start | bytes 1572868
  100.5 2.0 %collective-permute-start.10 = (f32[2,128,512]{2,1,0:T(8,128)S(1)}, f32[2,128,512]{2,1,0:T(8,128)S(1)}, u32[]{:S(2)}, u32[]{:S(2)}) collective-permute-start(f32[2,128,512]{2,1,0:T(8,128)S(1)} %get-tuple-element.46), channel_id=1, source_target_pairs={{0,2},{1,3},{2,0},{3,1},{4,6},{5,7},{6,4},{7,5},{8,10},{9,11},{10,... | collective-permute-start | bytes 1572872 | tf_op jit(solution)/shard_map/ppermute | solution.py:700
  100.7 4.6 %collective-permute-start.13 = (f32[2,128,512]{2,1,0:T(8,128)S(1)}, f32[2,128,512]{2,1,0:T(8,128)S(1)}, u32[]{:S(2)}, u32[]{:S(2)}) collective-permute-start(f32[2,128,512]{2,1,0:T(8,128)S(1)} %get-tuple-element.48), channel_id=1, source_target_pairs={{0,2},{1,3},{2,0},{3,1},{4,6},{5,7},{6,4},{7,5},{8,10},{9,11},{10,... | collective-permute-start | bytes 1572872 | tf_op jit(solution)/shard_map/ppermute | solution.py:700
  103.5 8.4 %collective-permute-start.11 = (f32[2,4,16,512]{3,2,1,0:T(8,128)S(1)}, f32[2,4,16,512]{3,2,1,0:T(8,128)S(1)}, u32[]{:S(2)}, u32[]{:S(2)}) collective-permute-start(f32[2,4,16,512]{3,2,1,0:T(8,128)S(1)} %add_bitcast_fusion.1), channel_id=1, source_target_pairs={{0,4},{1,5},{2,6},{3,7},{4,0},{5,1},{6,2},{7,3},{8,12},{9,13},{10,... | collective-permute-start | bytes 786440 | tf_op jit(solution)/shard_map/ppermute | solution.py:700
  106.3 8.5 %collective-permute-start.14 = (f32[2,4,16,512]{3,2,1,0:T(8,128)S(1)}, f32[2,4,16,512]{3,2,1,0:T(8,128)S(1)}, u32[]{:S(2)}, u32[]{:S(2)}) collective-permute-start(f32[2,4,16,512]{3,2,1,0:T(8,128)S(1)} %add_bitcast_fusion), channel_id=1, source_target_pairs={{0,1},{1,0},{2,3},{3,2},{4,5},{5,4},{6,7},{7,6},{8,9},{9,8},{10,11... | collective-permute-start | bytes 786440 | tf_op jit(solution)/shard_map/ppermute | solution.py:700
  113.0 5.0 %collective-permute-start.12 = (f32[4,16,512]{2,1,0:T(8,128)S(1)}, f32[4,16,512]{2,1,0:T(8,128)S(1)}, u32[]{:S(2)}, u32[]{:S(2)}) collective-permute-start(f32[4,16,512]{2,1,0:T(8,128)S(1)} %dynamic-slice_bitcast_fusion.1), channel_id=1, source_target_pairs={{0,1},{1,0},{2,3},{3,2},{4,5},{5,4},{6,7},{7,6},{8,9},{9,8},{10,11... | collective-permute-start | bytes 393224 | tf_op jit(solution)/shard_map/ppermute | solution.py:700
  114.9 5.0 %collective-permute-start.15 = (f32[4,16,512]{2,1,0:T(8,128)S(1)}, f32[4,16,512]{2,1,0:T(8,128)S(1)}, u32[]{:S(2)}, u32[]{:S(2)}) collective-permute-start(f32[4,16,512]{2,1,0:T(8,128)S(1)} %dynamic-slice_bitcast_fusion), channel_id=1, source_target_pairs={{0,4},{1,5},{2,6},{3,7},{4,0},{5,1},{6,2},{7,3},{8,12},{9,13},{10,... | collective-permute-start | bytes 393224 | tf_op jit(solution)/shard_map/ppermute | solution.py:700
  120.0 5.0 %collective-permute-start.16 = (f32[2,16,512]{2,1,0:T(8,128)S(1)}, f32[2,16,512]{2,1,0:T(8,128)S(1)}, u32[]{:S(2)}, u32[]{:S(2)}) collective-permute-start(f32[2,16,512]{2,1,0:T(8,128)S(1)} %get-tuple-element.55), channel_id=1, source_target_pairs={{0,8},{1,9},{2,10},{3,11},{4,12},{5,13},{6,14},{7,15},{8,0},{9,1},... | collective-permute-start | bytes 196616 | tf_op jit(solution)/shard_map/ppermute | solution.py:700
  121.7 6.2 %collective-permute-start.18 = (f32[2,16,512]{2,1,0:T(8,128)S(1)}, f32[2,16,512]{2,1,0:T(8,128)S(1)}, u32[]{:S(2)}, u32[]{:S(2)}) collective-permute-start(f32[2,16,512]{2,1,0:T(8,128)S(1)} %get-tuple-element.56), channel_id=1, source_target_pairs={{0,24},{1,25},{2,26},{3,27},{4,28},{5,29},{6,30},{7,31},{8,16},{9,... | collective-permute-start | bytes 196616 | tf_op jit(solution)/shard_map/ppermute | solution.py:700
  124.1 6.1 %collective-permute-start.17 = (f32[2,16,512]{2,1,0:T(8,128)S(1)}, f32[2,16,512]{2,1,0:T(8,128)S(1)}, u32[]{:S(2)}, u32[]{:S(2)}) collective-permute-start(f32[2,16,512]{2,1,0:T(8,128)S(1)} %get-tuple-element.57), channel_id=1, source_target_pairs={{0,16},{1,17},{2,18},{3,19},{4,20},{5,21},{6,22},{7,23},{8,24},{9,... | collective-permute-start | bytes 196616 | tf_op jit(solution)/shard_map/ppermute | solution.py:700
  131.1 5.8 %collective-permute-start.21 = (f32[16,512]{1,0:T(8,128)S(1)}, f32[16,512]{1,0:T(8,128)S(1)}, u32[]{:S(2)}, u32[]{:S(2)}) collective-permute-start(f32[16,512]{1,0:T(8,128)S(1)} %multiply_subtract_fusion), channel_id=1, source_target_pairs={{0,24},{1,25},{2,26},{3,27},{4,28},{5,29},{6,30},{7,31},{8,16},{9,... | collective-permute-start | bytes 98312 | tf_op jit(solution)/shard_map/ppermute | solution.py:700
  132.6 5.1 %collective-permute-start.20 = (f32[16,512]{1,0:T(8,128)S(1)}, f32[16,512]{1,0:T(8,128)S(1)}, u32[]{:S(2)}, u32[]{:S(2)}) collective-permute-start(f32[16,512]{1,0:T(8,128)S(1)} %multiply_subtract_fusion), channel_id=1, source_target_pairs={{0,16},{1,17},{2,18},{3,19},{4,20},{5,21},{6,22},{7,23},{8,24},{9,... | collective-permute-start | bytes 98312 | tf_op jit(solution)/shard_map/ppermute | solution.py:700
  132.6 5.2 %collective-permute-start.19 = (f32[16,512]{1,0:T(8,128)S(1)}, f32[16,512]{1,0:T(8,128)S(1)}, u32[]{:S(2)}, u32[]{:S(2)}) collective-permute-start(f32[16,512]{1,0:T(8,128)S(1)} %multiply_subtract_fusion), channel_id=1, source_target_pairs={{0,8},{1,9},{2,10},{3,11},{4,12},{5,13},{6,14},{7,15},{8,0},{9,1},... | collective-permute-start | bytes 98312 | tf_op jit(solution)/shard_map/ppermute | solution.py:700
  137.9 5.0 %collective-permute-start.22 = (f32[4,16,512]{2,1,0:T(8,128)S(1)}, f32[4,16,512]{2,1,0:T(8,128)S(1)}, u32[]{:S(2)}, u32[]{:S(2)}) collective-permute-start(f32[4,16,512]{2,1,0:T(8,128)S(1)} %bitcast.117), channel_id=1, source_target_pairs={{0,4},{1,5},{2,6},{3,7},{4,0},{5,1},{6,2},{7,3},{8,12},{9,13},{10,... | collective-permute-start | bytes 393224 | tf_op jit(solution)/shard_map/ppermute | solution.py:700
  143.0 1.6 %collective-permute-start.23 = (f32[2,4,16,512]{3,2,1,0:T(8,128)S(1)}, f32[2,4,16,512]{3,2,1,0:T(8,128)S(1)}, u32[]{:S(2)}, u32[]{:S(2)}) collective-permute-start(f32[2,4,16,512]{3,2,1,0:T(8,128)S(1)} %reverse_select_fusion.3), channel_id=1, source_target_pairs={{0,2},{1,3},{2,0},{3,1},{4,6},{5,7},{6,4},{7,5},{8,10},{9,11},{10,... | collective-permute-start | bytes 786440 | tf_op jit(solution)/shard_map/ppermute | solution.py:700

commit v2 on v1

--- a/solution.py
+++ b/solution.py
@@ -724,9 +724,9 @@
         (1 - space_index).reshape(1), (backward_fields,), ((0, True),), matrix, turn, True
     )
     got_backward = send(sent_backward, to_space)
-    quarter = half // 4
+    eighth = half // 8
     part = lax.dynamic_slice_in_dim(
-        phase, after(core_index * 2 + x_index, sent_backward) * quarter, quarter, axis=0
+        phase, after(core_index * 4 + x_index * 2 + z_index % 2, sent_backward) * eighth, eighth, axis=0
     )
     other_part = send(part, to_space)
     last_backward, last_forward = rows_call(
@@ -751,7 +751,7 @@
     )
 
     other_part = after(other_part, own_odd)
-    other_phase = share(share(other_part, x_index, to_x), core_index, to_core)
+    other_phase = share(share(share(other_part, z_index % 2, to_z[1]), x_index, to_x), core_index, to_core)
     whole_phase = swap_if(
         space_index, jnp.stack([phase, other_phase.reshape(half, pixels)])
     ).reshape(pixels, pixels)

time: 146 us -> 145 us (level)
  waiting for transfers between devices: 53.4 us -> 49.9 us
    ppermute x24 -> x25, waiting for transfers between devices: 53.4 us -> 49.9 us  [send(): return lax.ppermute(value, axes, pairs)]
    ppermute x24 -> x25, starting transfers between devices: 27.1 us -> 28.3 us  [send(): return lax.ppermute(value, axes, pairs)]
  transfers between devices with their start and end apart: 24 -> 25, of which waited for: 16 -> 16; matrix products, arithmetic and copies ran while one was open for 11% -> 11% of each run, Pallas kernels for 23% -> 23%
where the time goes in v2:
time: 145 us; the launch traced here: 144 us
  waiting for transfers between devices  49.9 us (34%)
  Pallas kernels  42.9 us (30%)
  starting transfers between devices  28.3 us (20%)
  other arithmetic  16.6 us (11%)
  local copies, waits for them, and re-layouts  5.77 us (4%)
    ppermute x25, waiting for transfers between devices, send(): return lax.ppermute(value, axes, pairs)  49.9 us
    ppermute x25, starting transfers between devices, send(): return lax.ppermute(value, axes, pairs)  28.3 us
    pallas_call x4, Pallas kernels, rows_call(): pl.pallas_call(kernel, out_shape=tuple(shapes), in_specs=[in_smem()] + [p...  15.7 us
    pallas_call x1, Pallas kernels, back_call(): pl.pallas_call(back_kernel, out_shape=jax.ShapeDtypeStruct((2, 2 * half,...  8 us
    pallas_call x1, Pallas kernels, shared_call(): pl.pallas_call(shared_kernel, out_shape=(part, part), in_specs=[in_smem()...  7.85 us
    pallas_call x1, Pallas kernels, final_call(): pl.pallas_call(final_kernel, out_shape=(part,) * 2 + (pltpu.HBM(part.shap...  6.46 us
    unnamed x34, local copies, waits for them, and re-layouts  4.63 us
    pallas_call x1, Pallas kernels, even_call(): pl.pallas_call(even_kernel, out_shape=jax.ShapeDtypeStruct((2, 2 * half,...  4.34 us
  transfers between devices with their start and end apart: 25, of which 16 were waited for; matrix products, arithmetic and copies ran while one was open for 11% of the time, Pallas kernels for 23%

profile of v2, /device:TPU:0, one launch (start us, length us, event | category | flops | bytes accessed | tf_op | source)
XLA Modules:
  0.0 144.0 jit_solution(12870583757917737910)
XLA Ops:
  0.0 3.7 %rows.4 = f32[2,2,256,256]{3,2,1,0:T(8,128)} custom-call(s32[1]{0:T(128)} %bitcast.2.index, f32[2,3,256,512]{3,2,1,0:T(8,128)} %refs_0_.7, bf16[2,512,512]{2,1,0:T(8,128)(2,1)} %constant.211.clone.refs_1_.refs_2_.matrix, f32[2,256]{1,0:T(2,128)} %constant.212.clone.refs_2_.refs_3_.turn), custom_call_target="tpu_custom_call" | custom-call | tf_op jit(solution)/shard_map/rows/pallas_call | solution.py:540
  3.7 3.1 %collective-permute-start.2 = (f32[2,2,256,256]{3,2,1,0:T(8,128)}, f32[2,2,256,256]{3,2,1,0:T(8,128)}, u32[]{:S(2)}, u32[]{:S(2)}) collective-permute-start(f32[2,2,256,256]{3,2,1,0:T(8,128)} %rows.4), channel_id=1, source_target_pairs={{0,1},{1,0},{2,3},{3,2},{4,5},{5,4},{6,7},{7,6},{8,9},{9,8},{10,11... | collective-permute-start | bytes 3145736 | tf_op jit(solution)/shard_map/ppermute | solution.py:700
  7.7 4.7 %rows.5 = (f32[2,2,256,256]{3,2,1,0:T(8,128)}, f32[2,2,256,256]{3,2,1,0:T(8,128)S(1)}) custom-call(s32[2]{0:T(128)S(1)} %broadcast.336.index, f32[2,3,256,512]{3,2,1,0:T(8,128)} %refs_0_.7, f32[2,3,256,512]{3,2,1,0:T(8,128)} %refs_1_.5, bf16[2,512,512]{2,1,0:T(8,128)(2,1)S(1)} %copy-done, f32[2,256]{1,0:T(2,128)S(1)} %copy-done.12), custom_call_target="tpu_custom_call" | custom-call | tf_op jit(solution)/shard_map/rows/pallas_call | solution.py:540
  12.6 3.3 %rows.6 = (f32[2,256,256]{2,1,0:T(8,128)}, f32[2,256,256]{2,1,0:T(8,128)}) custom-call(s32[1]{0:T(128)} %bitcast.2.index, f32[2,3,256,512]{3,2,1,0:T(8,128)} %refs_1_.5, bf16[2,512,512]{2,1,0:T(8,128)(2,1)S(1)} %copy-done, f32[2,256]{1,0:T(2,128)S(1)} %copy-done.12), custom_call_target="tpu_custom_call" | custom-call | tf_op jit(solution)/shard_map/rows/pallas_call | solution.py:540
  15.8 2.0 %collective-permute-start.9 = (f32[2,256,256]{2,1,0:T(8,128)}, f32[2,256,256]{2,1,0:T(8,128)}, u32[]{:S(2)}, u32[]{:S(2)}) collective-permute-start(f32[2,256,256]{2,1,0:T(8,128)} %get-tuple-element.43), channel_id=1, source_target_pairs={{0,1},{1,0},{2,3},{3,2},{4,5},{5,4},{6,7},{7,6},{8,9},{9,8},{10,11... | collective-permute-start | bytes 1572872 | tf_op jit(solution)/shard_map/ppermute | solution.py:700
  19.0 2.9 %fusion.20 = (f32[2,256,256]{2,1,0:T(8,128)}, f32[2,256,256]{2,1,0:T(8,128)}, f32[2,256,256]{2,1,0:T(8,128)S(1)}, f32[2,256,256]{2,1,0:T(8,128)S(1)}) fusion(f32[256]{0:T(256)S(1)} %bitcast.140, f32[2,256]{1,0:T(2,128)S(1)} %fusion.43, f32[256]{0:T(256)S(1)} %bitcast.141), kind=kLoop, calls=%fused_computation.52 | loop fusion | flops 12058624 | bytes 2101248 | tf_op jit(solution)/shard_map/div | solution.py:670
  21.9 2.8 %broadcast_select_fusion = (f32[2,2,256,256]{3,2,1,0:T(8,128)}, f32[2,2,256,256]{3,2,1,0:T(8,128)}) fusion(f32[2,2,256,256]{3,2,1,0:T(8,128)S(1)} %get-tuple-element.32, f32[2,2,256,256]{3,2,1,0:T(8,128)} %collective-permute-done, pred[]{:T(512)S(6)} %eq.143), kind=kLoop, calls=%fused_computation.75 | loop fusion | flops 524288 | bytes 4194305 | tf_op jit(solution)/shard_map/jit(_where)/select_n | solution.py:743
  24.7 4.0 %rows.7 = (f32[2,2,256,256]{3,2,1,0:T(8,128)S(1)}, f32[2,256,256]{2,1,0:T(8,128)S(1)}, f32[2,256,256]{2,1,0:T(8,128)S(1)}) custom-call(s32[2]{0:T(128)S(1)} %pad_add_fusion.index, f32[2,3,256,512]{3,2,1,0:T(8,128)} %refs_0_.7, f32[2,3,256,512]{3,2,1,0:T(8,128)} %refs_1_.5, bf16[2,512,512]{2,1,0:T(8,128)(2,1)S(1)} %copy-done, f32[2,256]{1,0:T(2,128)S(1)} %copy-done.12), custom_call_target="tpu_custom_call" | custom-call | tf_op jit(solution)/shard_map/rows/pallas_call | solution.py:540
  28.7 1.0 copy-done.6
  29.7 2.7 %collective-permute-done.5 = f32[32,512]{1,0:T(8,128)S(1)} collective-permute-done((f32[32,512]{1,0:T(8,128)S(1)}, f32[32,512]{1,0:T(8,128)S(1)}, u32[]{:S(2)}, u32[]{:S(2)}) %collective-permute-start.5) | collective-permute-done | bytes 65568 | tf_op jit(solution)/shard_map/ppermute | solution.py:700
  32.4 2.1 %collective-permute-start.6 = (f32[32,512]{1,0:T(8,128)S(1)}, f32[32,512]{1,0:T(8,128)S(1)}, u32[]{:S(2)}, u32[]{:S(2)}) collective-permute-start(f32[32,512]{1,0:T(8,128)S(1)} %collective-permute-done.5), channel_id=1, source_target_pairs={{0,8},{1,9},{2,10},{3,11},{4,12},{5,13},{6,14},{7,15},{8,0},{9,1},... | collective-permute-start | bytes 196616 | tf_op jit(solution)/shard_map/ppermute | solution.py:700
  34.5 1.1 reduce-precision_convert_fusion
  35.6 1.5 %collective-permute-start.3 = (f32[2,2,256,256]{3,2,1,0:T(8,128)}, f32[2,2,256,256]{3,2,1,0:T(8,128)}, u32[]{:S(2)}, u32[]{:S(2)}) collective-permute-start(f32[2,2,256,256]{3,2,1,0:T(8,128)} %get-tuple-element.50), channel_id=1, source_target_pairs={{0,1},{1,0},{2,3},{3,2},{4,5},{5,4},{6,7},{7,6},{8,9},{9,8},{10,11... | collective-permute-start | bytes 3145736 | tf_op jit(solution)/shard_map/ppermute | solution.py:700
  37.2 1.6 %collective-permute-start.7 = (f32[2,32,512]{2,1,0:T(8,128)S(1)}, f32[2,32,512]{2,1,0:T(8,128)S(1)}, u32[]{:S(2)}, u32[]{:S(2)}) collective-permute-start(f32[2,32,512]{2,1,0:T(8,128)S(1)} %reverse_select_fusion.9), channel_id=1, source_target_pairs={{0,4},{1,5},{2,6},{3,7},{4,0},{5,1},{6,2},{7,3},{8,12},{9,13},{10,... | collective-permute-start | bytes 393224 | tf_op jit(solution)/shard_map/ppermute | solution.py:700
  38.8 3.4 %collective-permute-done.7 = f32[2,32,512]{2,1,0:T(8,128)S(1)} collective-permute-done((f32[2,32,512]{2,1,0:T(8,128)S(1)}, f32[2,32,512]{2,1,0:T(8,128)S(1)}, u32[]{:S(2)}, u32[]{:S(2)}) %collective-permute-start.7) | collective-permute-done | bytes 131104 | tf_op jit(solution)/shard_map/ppermute | solution.py:700
  43.4 1.0 copy-done.1
  44.4 1.0 copy-done.3
  45.5 1.2 copy-done.7
  46.7 8.0 %back.1.returned = f32[2,512,512]{2,1,0:T(8,128)S(1)} custom-call(f32[2,2,256,256]{3,2,1,0:T(8,128)S(1)} %copy-done.7, f32[2,2,256,256]{3,2,1,0:T(8,128)} %collective-permute-done.2.other, bf16[2,512,512]{2,1,0:T(8,128)(2,1)S(1)} %copy-done, bf16[2,512,512]{2,1,0:T(8,128)(2,1)S(1)} %pad_maximum_fusion.2.turned, f32[2,256]{1,0:T(2,128)S(1)} %copy-done.12, ...), custom_call_target="tpu_custom_call" | custom-call | tf_op jit(solution)/shard_map/back/pallas_call | solution.py:558
  54.8 1.1 pad_maximum_fusion.4
  55.9 20.7 %collective-permute-done.3.other = f32[2,2,256,256]{3,2,1,0:T(8,128)} collective-permute-done((f32[2,2,256,256]{3,2,1,0:T(8,128)}, f32[2,2,256,256]{3,2,1,0:T(8,128)}, u32[]{:S(2)}, u32[]{:S(2)}) %collective-permute-start.3) | collective-permute-done | bytes 1048608 | tf_op jit(solution)/shard_map/ppermute | solution.py:700
  76.6 7.9 %shared.1 = (f32[2,256,512]{2,1,0:T(8,128)S(1)}, f32[2,256,512]{2,1,0:T(8,128)S(1)}) custom-call(s32[1]{0:T(128)} %bitcast.place, f32[1]{0:T(128)} %bitcast.3.sign, f32[2,2,256,256]{3,2,1,0:T(8,128)S(1)} %copy-done.5, f32[2,2,256,256]{3,2,1,0:T(8,128)} %collective-permute-done.3.other, bf16[2,512,512]{2,1,0:T(8,128)(2,1)S(1)} %copy-done, ...), custom_call_target="tpu_custom_call" | custom-call | tf_op jit(solution)/shard_map/shared/pallas_call | solution.py:586
  84.8 1.3 negate_select_fusion.1
  86.3 0.9 collective-permute-done.4.other
  88.2 4.3 %even.1 = f32[2,512,256]{2,1,0:T(8,128)S(1)} custom-call(f32[2,256,256]{2,1,0:T(8,128)S(1)} %copy-done.9, f32[2,256,256]{2,1,0:T(8,128)} %collective-permute-done.9.other, bf16[2,512,512]{2,1,0:T(8,128)(2,1)S(1)} %copy-done, bf16[2,512,512]{2,1,0:T(8,128)(2,1)S(1)} %pad_maximum_fusion.2.turned, f32[2,256,128]{2,1,0:T(8,128)S(1)} %broadcast_in_dim.4.turn_in, ...), custom_call_target="tpu_custom_call" | custom-call | tf_op jit(solution)/shard_map/even/pallas_call | solution.py:571
  92.6 6.5 %final.1 = (f32[2,128,512]{2,1,0:T(8,128)S(1)}, f32[2,128,512]{2,1,0:T(8,128)S(1)}, f32[2,128,512]{2,1,0:T(8,128)}, f32[2,128,512]{2,1,0:T(8,128)}) custom-call(s32[1]{0:T(128)} %bitcast.place, f32[2,256,256]{2,1,0:T(8,128)S(1)} %copy-done.11, f32[2,256,256]{2,1,0:T(8,128)} %collective-permute-done.1.other, f32[2,512,256]{2,1,0:T(8,128)S(1)} %even.1, ...), custom_call_target="tpu_custom_call" | custom-call | tf_op jit(solution)/shard_map/final/pallas_call | solution.py:614
  99.7 1.4 collective-permute-done.11
  101.1 1.0 add_bitcast_fusion.1
  102.1 1.8 %collective-permute-start.12 = (f32[2,4,16,512]{3,2,1,0:T(8,128)S(1)}, f32[2,4,16,512]{3,2,1,0:T(8,128)S(1)}, u32[]{:S(2)}, u32[]{:S(2)}) collective-permute-start(f32[2,4,16,512]{3,2,1,0:T(8,128)S(1)} %add_bitcast_fusion.1), channel_id=1, source_target_pairs={{0,4},{1,5},{2,6},{3,7},{4,0},{5,1},{6,2},{7,3},{8,12},{9,13},{10,... | collective-permute-start | bytes 786440 | tf_op jit(solution)/shard_map/ppermute | solution.py:700
  103.9 1.0 add_bitcast_fusion
  104.9 1.6 %collective-permute-start.15 = (f32[2,4,16,512]{3,2,1,0:T(8,128)S(1)}, f32[2,4,16,512]{3,2,1,0:T(8,128)S(1)}, u32[]{:S(2)}, u32[]{:S(2)}) collective-permute-start(f32[2,4,16,512]{3,2,1,0:T(8,128)S(1)} %add_bitcast_fusion), channel_id=1, source_target_pairs={{0,1},{1,0},{2,3},{3,2},{4,5},{5,4},{6,7},{7,6},{8,9},{9,8},{10,11... | collective-permute-start | bytes 786440 | tf_op jit(solution)/shard_map/ppermute | solution.py:700
  106.5 4.0 %collective-permute-done.12 = f32[2,4,16,512]{3,2,1,0:T(8,128)S(1)} collective-permute-done((f32[2,4,16,512]{3,2,1,0:T(8,128)S(1)}, f32[2,4,16,512]{3,2,1,0:T(8,128)S(1)}, u32[]{:S(2)}, u32[]{:S(2)}) %collective-permute-start.12) | collective-permute-done | bytes 262176 | tf_op jit(solution)/shard_map/ppermute | solution.py:700
  110.5 1.0 fusion.30
  111.5 1.8 %collective-permute-start.13 = (f32[4,16,512]{2,1,0:T(8,128)S(1)}, f32[4,16,512]{2,1,0:T(8,128)S(1)}, u32[]{:S(2)}, u32[]{:S(2)}) collective-permute-start(f32[4,16,512]{2,1,0:T(8,128)S(1)} %dynamic-slice_bitcast_fusion.1), channel_id=1, source_target_pairs={{0,1},{1,0},{2,3},{3,2},{4,5},{5,4},{6,7},{7,6},{8,9},{9,8},{10,11... | collective-permute-start | bytes 393224 | tf_op jit(solution)/shard_map/ppermute | solution.py:700
  113.5 1.6 %collective-permute-start.16 = (f32[4,16,512]{2,1,0:T(8,128)S(1)}, f32[4,16,512]{2,1,0:T(8,128)S(1)}, u32[]{:S(2)}, u32[]{:S(2)}) collective-permute-start(f32[4,16,512]{2,1,0:T(8,128)S(1)} %dynamic-slice_bitcast_fusion), channel_id=1, source_target_pairs={{0,4},{1,5},{2,6},{3,7},{4,0},{5,1},{6,2},{7,3},{8,12},{9,13},{10,... | collective-permute-start | bytes 393224 | tf_op jit(solution)/shard_map/ppermute | solution.py:700
  115.0 1.6 %collective-permute-done.13 = f32[4,16,512]{2,1,0:T(8,128)S(1)} collective-permute-done((f32[4,16,512]{2,1,0:T(8,128)S(1)}, f32[4,16,512]{2,1,0:T(8,128)S(1)}, u32[]{:S(2)}, u32[]{:S(2)}) %collective-permute-start.13) | collective-permute-done | bytes 131104 | tf_op jit(solution)/shard_map/ppermute | solution.py:700
  116.6 1.9 %collective-permute-done.16 = f32[4,16,512]{2,1,0:T(8,128)S(1)} collective-permute-done((f32[4,16,512]{2,1,0:T(8,128)S(1)}, f32[4,16,512]{2,1,0:T(8,128)S(1)}, u32[]{:S(2)}, u32[]{:S(2)}) %collective-permute-start.16) | collective-permute-done | bytes 131104 | tf_op jit(solution)/shard_map/ppermute | solution.py:700
  118.6 1.6 %collective-permute-start.17 = (f32[2,16,512]{2,1,0:T(8,128)S(1)}, f32[2,16,512]{2,1,0:T(8,128)S(1)}, u32[]{:S(2)}, u32[]{:S(2)}) collective-permute-start(f32[2,16,512]{2,1,0:T(8,128)S(1)} %get-tuple-element.55), channel_id=1, source_target_pairs={{0,8},{1,9},{2,10},{3,11},{4,12},{5,13},{6,14},{7,15},{8,0},{9,1},... | collective-permute-start | bytes 196616 | tf_op jit(solution)/shard_map/ppermute | solution.py:700
  120.2 2.5 %collective-permute-start.19 = (f32[2,16,512]{2,1,0:T(8,128)S(1)}, f32[2,16,512]{2,1,0:T(8,128)S(1)}, u32[]{:S(2)}, u32[]{:S(2)}) collective-permute-start(f32[2,16,512]{2,1,0:T(8,128)S(1)} %get-tuple-element.56), channel_id=1, source_target_pairs={{0,24},{1,25},{2,26},{3,27},{4,28},{5,29},{6,30},{7,31},{8,16},{9,... | collective-permute-start | bytes 196616 | tf_op jit(solution)/shard_map/ppermute | solution.py:700
  123.6 2.8 %collective-permute-done.19 = f32[2,16,512]{2,1,0:T(8,128)S(1)} collective-permute-done((f32[2,16,512]{2,1,0:T(8,128)S(1)}, f32[2,16,512]{2,1,0:T(8,128)S(1)}, u32[]{:S(2)}, u32[]{:S(2)}) %collective-permute-start.19) | collective-permute-done | bytes 65568 | tf_op jit(solution)/shard_map/ppermute | solution.py:700
  126.4 2.4 %collective-permute-done.18 = f32[2,16,512]{2,1,0:T(8,128)S(1)} collective-permute-done((f32[2,16,512]{2,1,0:T(8,128)S(1)}, f32[2,16,512]{2,1,0:T(8,128)S(1)}, u32[]{:S(2)}, u32[]{:S(2)}) %collective-permute-start.18) | collective-permute-done | bytes 65568 | tf_op jit(solution)/shard_map/ppermute | solution.py:700
  128.8 0.9 multiply_subtract_fusion
  129.7 1.5 %collective-permute-start.22 = (f32[16,512]{1,0:T(8,128)S(1)}, f32[16,512]{1,0:T(8,128)S(1)}, u32[]{:S(2)}, u32[]{:S(2)}) collective-permute-start(f32[16,512]{1,0:T(8,128)S(1)} %multiply_subtract_fusion), channel_id=1, source_target_pairs={{0,24},{1,25},{2,26},{3,27},{4,28},{5,29},{6,30},{7,31},{8,16},{9,... | collective-permute-start | bytes 98312 | tf_op jit(solution)/shard_map/ppermute | solution.py:700
  131.2 3.0 %collective-permute-start.20 = (f32[16,512]{1,0:T(8,128)S(1)}, f32[16,512]{1,0:T(8,128)S(1)}, u32[]{:S(2)}, u32[]{:S(2)}) collective-permute-start(f32[16,512]{1,0:T(8,128)S(1)} %multiply_subtract_fusion), channel_id=1, source_target_pairs={{0,8},{1,9},{2,10},{3,11},{4,12},{5,13},{6,14},{7,15},{8,0},{9,1},... | collective-permute-start | bytes 98312 | tf_op jit(solution)/shard_map/ppermute | solution.py:700
  134.2 1.3 collective-permute-done.22
  136.5 1.6 %collective-permute-start.23 = (f32[4,16,512]{2,1,0:T(8,128)S(1)}, f32[4,16,512]{2,1,0:T(8,128)S(1)}, u32[]{:S(2)}, u32[]{:S(2)}) collective-permute-start(f32[4,16,512]{2,1,0:T(8,128)S(1)} %bitcast.120), channel_id=1, source_target_pairs={{0,4},{1,5},{2,6},{3,7},{4,0},{5,1},{6,2},{7,3},{8,12},{9,13},{10,... | collective-permute-start | bytes 393224 | tf_op jit(solution)/shard_map/ppermute | solution.py:700
  138.0 3.5 %collective-permute-done.23 = f32[4,16,512]{2,1,0:T(8,128)S(1)} collective-permute-done((f32[4,16,512]{2,1,0:T(8,128)S(1)}, f32[4,16,512]{2,1,0:T(8,128)S(1)}, u32[]{:S(2)}, u32[]{:S(2)}) %collective-permute-start.23) | collective-permute-done | bytes 131104 | tf_op jit(solution)/shard_map/ppermute | solution.py:700
  141.7 1.5 %collective-permute-done.24 = f32[2,4,16,512]{3,2,1,0:T(8,128)S(1)} collective-permute-done((f32[2,4,16,512]{3,2,1,0:T(8,128)S(1)}, f32[2,4,16,512]{3,2,1,0:T(8,128)S(1)}, u32[]{:S(2)}, u32[]{:S(2)}) %collective-permute-start.24) | collective-permute-done | bytes 262176 | tf_op jit(solution)/shard_map/ppermute | solution.py:700
  (96 shorter events, 8.6 us)
Async XLA Ops:
  0.0 7.7 %copy-start = (bf16[2,512,512]{2,1,0:T(8,128)(2,1)S(1)}, bf16[2,512,512]{2,1,0:T(8,128)(2,1)}, u32[]{:S(2)}) copy-start(bf16[2,512,512]{2,1,0:T(8,128)(2,1)} %constant.211.clone.refs_1_.refs_2_.matrix) | copy-start | bytes 3145732
  0.0 7.7 %copy-start.12 = (f32[2,256]{1,0:T(2,128)S(1)}, f32[2,256]{1,0:T(2,128)}, u32[]{:S(2)}) copy-start(f32[2,256]{1,0:T(2,128)} %constant.212.clone.refs_2_.refs_3_.turn) | copy-start | bytes 6148
  3.7 39.4 %collective-permute-start.2 = (f32[2,2,256,256]{3,2,1,0:T(8,128)}, f32[2,2,256,256]{3,2,1,0:T(8,128)}, u32[]{:S(2)}, u32[]{:S(2)}) collective-permute-start(f32[2,2,256,256]{3,2,1,0:T(8,128)} %rows.4), channel_id=1, source_target_pairs={{0,1},{1,0},{2,3},{3,2},{4,5},{5,4},{6,7},{7,6},{8,9},{9,8},{10,11... | collective-permute-start | bytes 3145736 | tf_op jit(solution)/shard_map/ppermute | solution.py:700
  7.6 24.8 %collective-permute-start.5 = (f32[32,512]{1,0:T(8,128)S(1)}, f32[32,512]{1,0:T(8,128)S(1)}, u32[]{:S(2)}, u32[]{:S(2)}) collective-permute-start(f32[32,512]{1,0:T(8,128)S(1)} %constant_dynamic-slice_fusion), channel_id=1, source_target_pairs={{0,1},{1,0},{2,3},{3,2},{4,5},{5,4},{6,7},{7,6},{8,9},{9,8},{10,11... | collective-permute-start | bytes 196616 | tf_op jit(solution)/shard_map/ppermute | solution.py:700
  12.5 9.4 %collective-permute-start = (f32[2,2,256,256]{3,2,1,0:T(8,128)}, f32[2,2,256,256]{3,2,1,0:T(8,128)}, u32[]{:S(2)}, u32[]{:S(2)}) collective-permute-start(f32[2,2,256,256]{3,2,1,0:T(8,128)} %get-tuple-element.29), channel_id=1, source_target_pairs={{0,2},{1,3},{2,0},{3,1},{4,6},{5,7},{6,4},{7,5},{8,10},{9,11},{10,... | collective-permute-start | bytes 3145736 | tf_op jit(solution)/shard_map/ppermute | solution.py:700
  15.8 72.1 %collective-permute-start.9 = (f32[2,256,256]{2,1,0:T(8,128)}, f32[2,256,256]{2,1,0:T(8,128)}, u32[]{:S(2)}, u32[]{:S(2)}) collective-permute-start(f32[2,256,256]{2,1,0:T(8,128)} %get-tuple-element.43), channel_id=1, source_target_pairs={{0,1},{1,0},{2,3},{3,2},{4,5},{5,4},{6,7},{7,6},{8,9},{9,8},{10,11... | collective-permute-start | bytes 1572872 | tf_op jit(solution)/shard_map/ppermute | solution.py:700
  17.8 74.8 %collective-permute-start.1 = (f32[2,256,256]{2,1,0:T(8,128)}, f32[2,256,256]{2,1,0:T(8,128)}, u32[]{:S(2)}, u32[]{:S(2)}) collective-permute-start(f32[2,256,256]{2,1,0:T(8,128)} %get-tuple-element.31), channel_id=1, source_target_pairs={{0,1},{1,0},{2,3},{3,2},{4,5},{5,4},{6,7},{7,6},{8,9},{9,8},{10,11... | collective-permute-start | bytes 1572872 | tf_op jit(solution)/shard_map/ppermute | solution.py:700
  28.7 1.0 copy-start.6
  29.7 13.3 %copy-start.8 = (f32[2,256,256]{2,1,0:T(8,128)}, f32[2,256,256]{2,1,0:T(8,128)S(1)}, u32[]{:S(2)}) copy-start(f32[2,256,256]{2,1,0:T(8,128)S(1)} %get-tuple-element.42.own) | copy-start | bytes 1572868
  29.7 13.3 %copy-start.10 = (f32[2,256,256]{2,1,0:T(8,128)}, f32[2,256,256]{2,1,0:T(8,128)S(1)}, u32[]{:S(2)}) copy-start(f32[2,256,256]{2,1,0:T(8,128)S(1)} %get-tuple-element.34.own) | copy-start | bytes 1572868
  32.4 4.8 %collective-permute-start.6 = (f32[32,512]{1,0:T(8,128)S(1)}, f32[32,512]{1,0:T(8,128)S(1)}, u32[]{:S(2)}, u32[]{:S(2)}) collective-permute-start(f32[32,512]{1,0:T(8,128)S(1)} %collective-permute-done.5), channel_id=1, source_target_pairs={{0,8},{1,9},{2,10},{3,11},{4,12},{5,13},{6,14},{7,15},{8,0},{9,1},... | collective-permute-start | bytes 196616 | tf_op jit(solution)/shard_map/ppermute | solution.py:700
  35.6 7.3 %copy-start.13 = (bf16[1,512,512]{2,1,0:T(8,128)(2,1)S(1)}, bf16[1,512,512]{2,1,0:T(8,128)(2,1)}, u32[]{:S(2)}) copy-start(bf16[1,512,512]{2,1,0:T(8,128)(2,1)} %get-tuple-element.53) | copy-start | bytes 1572868
  35.6 7.4 %copy-start.14 = (bf16[1,512,512]{2,1,0:T(8,128)(2,1)S(1)}, bf16[1,512,512]{2,1,0:T(8,128)(2,1)}, u32[]{:S(2)}) copy-start(bf16[1,512,512]{2,1,0:T(8,128)(2,1)} %get-tuple-element.54) | copy-start | bytes 1572868
  35.6 41.0 %collective-permute-start.3 = (f32[2,2,256,256]{3,2,1,0:T(8,128)}, f32[2,2,256,256]{3,2,1,0:T(8,128)}, u32[]{:S(2)}, u32[]{:S(2)}) collective-permute-start(f32[2,2,256,256]{3,2,1,0:T(8,128)} %get-tuple-element.50), channel_id=1, source_target_pairs={{0,1},{1,0},{2,3},{3,2},{4,5},{5,4},{6,7},{7,6},{8,9},{9,8},{10,11... | collective-permute-start | bytes 3145736 | tf_op jit(solution)/shard_map/ppermute | solution.py:700
  37.2 5.0 %collective-permute-start.7 = (f32[2,32,512]{2,1,0:T(8,128)S(1)}, f32[2,32,512]{2,1,0:T(8,128)S(1)}, u32[]{:S(2)}, u32[]{:S(2)}) collective-permute-start(f32[2,32,512]{2,1,0:T(8,128)S(1)} %reverse_select_fusion.9), channel_id=1, source_target_pairs={{0,4},{1,5},{2,6},{3,7},{4,0},{5,1},{6,2},{7,3},{8,12},{9,13},{10,... | collective-permute-start | bytes 393224 | tf_op jit(solution)/shard_map/ppermute | solution.py:700
  43.0 11.8 %collective-permute-start.8 = (f32[2,2,32,512]{3,2,1,0:T(8,128)}, f32[2,2,32,512]{3,2,1,0:T(8,128)}, u32[]{:S(2)}, u32[]{:S(2)}) collective-permute-start(f32[2,2,32,512]{3,2,1,0:T(8,128)} %reverse_select_fusion.6), channel_id=1, source_target_pairs={{0,2},{1,3},{2,0},{3,1},{4,6},{5,7},{6,4},{7,5},{8,10},{9,11},{10,... | collective-permute-start | bytes 786440 | tf_op jit(solution)/shard_map/ppermute | solution.py:700
  43.4 1.0 copy-start.1
  44.4 1.0 copy-start.3
  45.5 1.2 copy-start.7
  54.7 21.9 %copy-start.5 = (f32[2,2,256,256]{3,2,1,0:T(8,128)S(1)}, f32[2,2,256,256]{3,2,1,0:T(8,128)}, u32[]{:S(2)}) copy-start(f32[2,2,256,256]{3,2,1,0:T(8,128)} %get-tuple-element.37.own) | copy-start | bytes 3145732
  76.6 8.0 %copy-start.15 = (f32[256,512]{1,0:T(8,128)S(1)}, f32[256,512]{1,0:T(8,128)}, u32[]{:S(2)}) copy-start(f32[256,512]{1,0:T(8,128)} %param.7) | copy-start | bytes 1572868
  84.5 2.7 %collective-permute-start.4 = (f32[2,256,512]{2,1,0:T(8,128)S(1)}, f32[2,256,512]{2,1,0:T(8,128)S(1)}, u32[]{:S(2)}, u32[]{:S(2)}) collective-permute-start(f32[2,256,512]{2,1,0:T(8,128)S(1)} %get-tuple-element.39), channel_id=1, source_target_pairs={{0,2},{1,3},{2,0},{3,1},{4,6},{5,7},{6,4},{7,5},{8,10},{9,11},{10,... | collective-permute-start | bytes 3145736 | tf_op jit(solution)/shard_map/ppermute | solution.py:700
  87.2 1.0 copy-start.9
  87.8 4.8 %collective-permute-start.10 = (f32[3,8,128]{2,1,0:T(8,128)S(1)}, f32[3,8,128]{2,1,0:T(8,128)S(1)}, u32[]{:S(2)}, u32[]{:S(2)}) collective-permute-start(f32[3,8,128]{2,1,0:T(8,128)S(1)} %get-tuple-element.41.sums_here), channel_id=1, source_target_pairs={{0,2},{1,3},{2,0},{3,1},{4,6},{5,7},{6,4},{7,5},{8,10},{9,11},{10,... | collective-permute-start | bytes 36872 | tf_op jit(solution)/shard_map/ppermute | solution.py:700
  87.9 4.7 %copy-start.2 = (f32[2,256,256]{2,1,0:T(8,128)S(1)}, f32[2,256,256]{2,1,0:T(8,128)}, u32[]{:S(2)}) copy-start(f32[2,256,256]{2,1,0:T(8,128)} %get-tuple-element.60.sin_odd.sin_part) | copy-start | bytes 1572868
  87.9 4.7 %copy-start.4 = (f32[2,256,256]{2,1,0:T(8,128)S(1)}, f32[2,256,256]{2,1,0:T(8,128)}, u32[]{:S(2)}) copy-start(f32[2,256,256]{2,1,0:T(8,128)} %get-tuple-element.61.cos_odd.cos_part) | copy-start | bytes 1572868
  87.9 4.7 %copy-start.11 = (f32[2,256,256]{2,1,0:T(8,128)S(1)}, f32[2,256,256]{2,1,0:T(8,128)}, u32[]{:S(2)}) copy-start(f32[2,256,256]{2,1,0:T(8,128)} %copy-done.10) | copy-start | bytes 1572868
  99.1 14.3 %copy-start.16 = (f32[2,128,512]{2,1,0:T(8,128)S(1)}, f32[2,128,512]{2,1,0:T(8,128)}, u32[]{:S(2)}) copy-start(f32[2,128,512]{2,1,0:T(8,128)} %get-tuple-element.47) | copy-start | bytes 1572868
  99.1 2.0 %collective-permute-start.11 = (f32[2,128,512]{2,1,0:T(8,128)S(1)}, f32[2,128,512]{2,1,0:T(8,128)S(1)}, u32[]{:S(2)}, u32[]{:S(2)}) collective-permute-start(f32[2,128,512]{2,1,0:T(8,128)S(1)} %get-tuple-element.46), channel_id=1, source_target_pairs={{0,2},{1,3},{2,0},{3,1},{4,6},{5,7},{6,4},{7,5},{8,10},{9,11},{10,... | collective-permute-start | bytes 1572872 | tf_op jit(solution)/shard_map/ppermute | solution.py:700
  99.3 4.6 %collective-permute-start.14 = (f32[2,128,512]{2,1,0:T(8,128)S(1)}, f32[2,128,512]{2,1,0:T(8,128)S(1)}, u32[]{:S(2)}, u32[]{:S(2)}) collective-permute-start(f32[2,128,512]{2,1,0:T(8,128)S(1)} %get-tuple-element.48), channel_id=1, source_target_pairs={{0,2},{1,3},{2,0},{3,1},{4,6},{5,7},{6,4},{7,5},{8,10},{9,11},{10,... | collective-permute-start | bytes 1572872 | tf_op jit(solution)/shard_map/ppermute | solution.py:700
  102.1 8.4 %collective-permute-start.12 = (f32[2,4,16,512]{3,2,1,0:T(8,128)S(1)}, f32[2,4,16,512]{3,2,1,0:T(8,128)S(1)}, u32[]{:S(2)}, u32[]{:S(2)}) collective-permute-start(f32[2,4,16,512]{3,2,1,0:T(8,128)S(1)} %add_bitcast_fusion.1), channel_id=1, source_target_pairs={{0,4},{1,5},{2,6},{3,7},{4,0},{5,1},{6,2},{7,3},{8,12},{9,13},{10,... | collective-permute-start | bytes 786440 | tf_op jit(solution)/shard_map/ppermute | solution.py:700
  104.9 8.5 %collective-permute-start.15 = (f32[2,4,16,512]{3,2,1,0:T(8,128)S(1)}, f32[2,4,16,512]{3,2,1,0:T(8,128)S(1)}, u32[]{:S(2)}, u32[]{:S(2)}) collective-permute-start(f32[2,4,16,512]{3,2,1,0:T(8,128)S(1)} %add_bitcast_fusion), channel_id=1, source_target_pairs={{0,1},{1,0},{2,3},{3,2},{4,5},{5,4},{6,7},{7,6},{8,9},{9,8},{10,11... | collective-permute-start | bytes 786440 | tf_op jit(solution)/shard_map/ppermute | solution.py:700
  111.5 5.0 %collective-permute-start.13 = (f32[4,16,512]{2,1,0:T(8,128)S(1)}, f32[4,16,512]{2,1,0:T(8,128)S(1)}, u32[]{:S(2)}, u32[]{:S(2)}) collective-permute-start(f32[4,16,512]{2,1,0:T(8,128)S(1)} %dynamic-slice_bitcast_fusion.1), channel_id=1, source_target_pairs={{0,1},{1,0},{2,3},{3,2},{4,5},{5,4},{6,7},{7,6},{8,9},{9,8},{10,11... | collective-permute-start | bytes 393224 | tf_op jit(solution)/shard_map/ppermute | solution.py:700
  113.5 5.0 %collective-permute-start.16 = (f32[4,16,512]{2,1,0:T(8,128)S(1)}, f32[4,16,512]{2,1,0:T(8,128)S(1)}, u32[]{:S(2)}, u32[]{:S(2)}) collective-permute-start(f32[4,16,512]{2,1,0:T(8,128)S(1)} %dynamic-slice_bitcast_fusion), channel_id=1, source_target_pairs={{0,4},{1,5},{2,6},{3,7},{4,0},{5,1},{6,2},{7,3},{8,12},{9,13},{10,... | collective-permute-start | bytes 393224 | tf_op jit(solution)/shard_map/ppermute | solution.py:700
  118.6 5.0 %collective-permute-start.17 = (f32[2,16,512]{2,1,0:T(8,128)S(1)}, f32[2,16,512]{2,1,0:T(8,128)S(1)}, u32[]{:S(2)}, u32[]{:S(2)}) collective-permute-start(f32[2,16,512]{2,1,0:T(8,128)S(1)} %get-tuple-element.55), channel_id=1, source_target_pairs={{0,8},{1,9},{2,10},{3,11},{4,12},{5,13},{6,14},{7,15},{8,0},{9,1},... | collective-permute-start | bytes 196616 | tf_op jit(solution)/shard_map/ppermute | solution.py:700
  120.2 6.2 %collective-permute-start.19 = (f32[2,16,512]{2,1,0:T(8,128)S(1)}, f32[2,16,512]{2,1,0:T(8,128)S(1)}, u32[]{:S(2)}, u32[]{:S(2)}) collective-permute-start(f32[2,16,512]{2,1,0:T(8,128)S(1)} %get-tuple-element.56), channel_id=1, source_target_pairs={{0,24},{1,25},{2,26},{3,27},{4,28},{5,29},{6,30},{7,31},{8,16},{9,... | collective-permute-start | bytes 196616 | tf_op jit(solution)/shard_map/ppermute | solution.py:700
  122.7 6.1 %collective-permute-start.18 = (f32[2,16,512]{2,1,0:T(8,128)S(1)}, f32[2,16,512]{2,1,0:T(8,128)S(1)}, u32[]{:S(2)}, u32[]{:S(2)}) collective-permute-start(f32[2,16,512]{2,1,0:T(8,128)S(1)} %get-tuple-element.57), channel_id=1, source_target_pairs={{0,16},{1,17},{2,18},{3,19},{4,20},{5,21},{6,22},{7,23},{8,24},{9,... | collective-permute-start | bytes 196616 | tf_op jit(solution)/shard_map/ppermute | solution.py:700
  129.7 5.8 %collective-permute-start.22 = (f32[16,512]{1,0:T(8,128)S(1)}, f32[16,512]{1,0:T(8,128)S(1)}, u32[]{:S(2)}, u32[]{:S(2)}) collective-permute-start(f32[16,512]{1,0:T(8,128)S(1)} %multiply_subtract_fusion), channel_id=1, source_target_pairs={{0,24},{1,25},{2,26},{3,27},{4,28},{5,29},{6,30},{7,31},{8,16},{9,... | collective-permute-start | bytes 98312 | tf_op jit(solution)/shard_map/ppermute | solution.py:700
  131.2 5.1 %collective-permute-start.21 = (f32[16,512]{1,0:T(8,128)S(1)}, f32[16,512]{1,0:T(8,128)S(1)}, u32[]{:S(2)}, u32[]{:S(2)}) collective-permute-start(f32[16,512]{1,0:T(8,128)S(1)} %multiply_subtract_fusion), channel_id=1, source_target_pairs={{0,16},{1,17},{2,18},{3,19},{4,20},{5,21},{6,22},{7,23},{8,24},{9,... | collective-permute-start | bytes 98312 | tf_op jit(solution)/shard_map/ppermute | solution.py:700
  131.2 5.2 %collective-permute-start.20 = (f32[16,512]{1,0:T(8,128)S(1)}, f32[16,512]{1,0:T(8,128)S(1)}, u32[]{:S(2)}, u32[]{:S(2)}) collective-permute-start(f32[16,512]{1,0:T(8,128)S(1)} %multiply_subtract_fusion), channel_id=1, source_target_pairs={{0,8},{1,9},{2,10},{3,11},{4,12},{5,13},{6,14},{7,15},{8,0},{9,1},... | collective-permute-start | bytes 98312 | tf_op jit(solution)/shard_map/ppermute | solution.py:700
  136.5 5.0 %collective-permute-start.23 = (f32[4,16,512]{2,1,0:T(8,128)S(1)}, f32[4,16,512]{2,1,0:T(8,128)S(1)}, u32[]{:S(2)}, u32[]{:S(2)}) collective-permute-start(f32[4,16,512]{2,1,0:T(8,128)S(1)} %bitcast.120), channel_id=1, source_target_pairs={{0,4},{1,5},{2,6},{3,7},{4,0},{5,1},{6,2},{7,3},{8,12},{9,13},{10,... | collective-permute-start | bytes 393224 | tf_op jit(solution)/shard_map/ppermute | solution.py:700
  141.6 1.6 %collective-permute-start.24 = (f32[2,4,16,512]{3,2,1,0:T(8,128)S(1)}, f32[2,4,16,512]{3,2,1,0:T(8,128)S(1)}, u32[]{:S(2)}, u32[]{:S(2)}) collective-permute-start(f32[2,4,16,512]{3,2,1,0:T(8,128)S(1)} %reverse_select_fusion.3), channel_id=1, source_target_pairs={{0,2},{1,3},{2,0},{3,1},{4,6},{5,7},{6,4},{7,5},{8,10},{9,11},{10,... | collective-permute-start | bytes 786440 | tf_op jit(solution)/shard_map/ppermute | solution.py:700
